TPU v7x, 32 devices: a whole 2x2x4 slice. The times are simulated.
32 devices in a mesh: groups: 2 (over y), tensor: 4 (over z), rows: 2 (over x), role: 2 (over core).
Axes of the slice: x: 2, y: 2, z: 4, core: 2. Of those that a mesh axis runs over, the one named last changes fastest.
Arguments:
- residual: bfloat16 [64, 8192], P(('groups', 'tensor'), ('rows', 'role')), parts along dimension 0, may hold values from -6 to 6
- attn_gain: float32 [8192], P(('rows', 'role')), may hold values from 0.1 to 1.9
- attn_proj: bfloat16 [3, 8192, 8192], P(None, ('rows', 'role'), 'tensor'), may hold values from -0.0625 to 0.0625
- cache_keys: bfloat16 [64, 32, 8192], P(('groups', 'rows', 'role'), None, 'tensor'), parts along dimension 0, may hold values from -600 to 600
- cache_values: bfloat16 [64, 32, 8192], P(('groups', 'rows', 'role'), None, 'tensor'), parts along dimension 0, may hold values from -6 to 6
- lengths: int32 [64], P(('groups', 'rows', 'role')), parts along dimension 0, may hold values from 1 to 32
- placement: int32 [64], P('groups'), parts along dimension 0, may hold values from 0 to 31, each once
- out_proj: bfloat16 [8192, 8192], P('tensor', ('rows', 'role')), may hold values from -0.0625 to 0.0625
- mix_gain: float32 [8192], P(('rows', 'role')), may hold values from 0.1 to 1.9
- mix_proj: bfloat16 [3, 8192, 8192], P(None, ('rows', 'role'), 'tensor'), may hold values from -0.0625 to 0.0625
- outer_taps: float32 [3, 3, 8192], P(None, None, 'tensor'), may hold values from -1 to 1
- outer_state: bfloat16 [2, 3, 64, 8192], P(None, None, ('groups', 'rows', 'role'), 'tensor'), parts along dimension 2, may hold values from -6 to 6
- inner_taps: float32 [3, 8192], P(None, 'tensor'), may hold values from -1 to 1
- inner_state: bfloat16 [2, 64, 8192], P(None, ('groups', 'rows', 'role'), 'tensor'), parts along dimension 1, may hold values from -6 to 6
Outputs:
- attended: bfloat16 [64, 8192], P(('groups', 'tensor'), ('rows', 'role')), parts along dimension 0
- gated: bfloat16 [64, 8192], P(('groups', 'rows', 'role'), 'tensor'), parts along dimension 0
There are 2 independent parts, one for each index of `groups`. A program takes and returns all parts, laid end to end along the dimension named above; an argument that names none is the same for every part. Nothing has to cross between parts.
Inputs may be any that keep to these rules, and one draw needn't show every extreme that they name: Cache slot s holds lengths[s] cached positions, the first of its 32. `placement`: each row has its own cache slot.
All inputs are finite; a program needn't handle non-finite values.
Results may differ from a plain program's by a relative error of at most 0.017.
Values may be sent and summed in bfloat16 or wider, within the bound.
No kernel may reach another device: no remote copies, remote signals or barrier semaphores. Data moves between devices by JAX's collectives and lax.ppermute only.
A program may use at most 128 MiB of HBM per device.

v0:
```python
import math

import jax
import jax.numpy as jnp
from jax import lax
from jax.sharding import PartitionSpec as P

D = 8192
HEAD_DIM = 128


def local(
    residual,
    attn_gain,
    attn_proj,
    cache_keys,
    cache_values,
    lengths,
    placement,
    out_proj,
    mix_gain,
    mix_proj,
    outer_taps,
    outer_state,
    inner_taps,
    inner_state,
):
    widened = residual.astype(jnp.float32)
    squares = lax.psum(jnp.sum(widened * widened, axis=1), ("rows", "role"))
    normed = (widened * lax.rsqrt(squares / D + 1e-05)[:, None] * attn_gain).astype(jnp.bfloat16)
    terms = jnp.einsum(
        "rd,jde->jre",
        lax.all_gather(normed, "tensor", axis=0, tiled=True),
        attn_proj,
        preferred_element_type=jnp.float32,
    )
    row_total = placement.shape[0]
    slot_count = lengths.shape[0]
    inverse = (
        jnp.zeros((row_total,), jnp.int32).at[placement].set(jnp.arange(row_total, dtype=jnp.int32))
    )
    full = lax.psum(terms, ("rows", "role"))
    first_slot = lax.axis_index(("rows", "role")) * slot_count
    owned_rows = lax.dynamic_slice_in_dim(inverse, first_slot, slot_count)
    sums = jnp.take(full, owned_rows, axis=1)
    triple = sums.astype(jnp.bfloat16)
    width_here = attn_proj.shape[2]
    head_count = width_here // HEAD_DIM
    positions = cache_keys.shape[1]
    query = triple[0].reshape(slot_count, head_count, HEAD_DIM)
    fresh_key = triple[1].reshape(slot_count, head_count, HEAD_DIM)
    fresh_value = triple[2].reshape(slot_count, head_count, HEAD_DIM)
    keys_local = cache_keys.reshape(slot_count, positions, head_count, HEAD_DIM)
    values_local = cache_values.reshape(slot_count, positions, head_count, HEAD_DIM)
    scale = 1.0 / math.sqrt(HEAD_DIM)
    scores = (
        jnp.einsum("shd,sphd->shp", query, keys_local, preferred_element_type=jnp.float32) * scale
    )
    own_score = (
        jnp.einsum("shd,shd->sh", query, fresh_key, preferred_element_type=jnp.float32) * scale
    )
    live = jnp.arange(positions, dtype=jnp.int32)[None, None, :] < lengths[:, None, None]
    top_score = jnp.maximum(jnp.max(jnp.where(live, scores, -jnp.inf), axis=2), own_score)
    probs = jnp.where(live, jnp.exp(scores - top_score[:, :, None]), 0.0)
    self_prob = jnp.exp(own_score - top_score)
    total = jnp.sum(probs, axis=2) + self_prob
    weights = (probs / total[:, :, None]).astype(jnp.bfloat16)
    self_weight = (self_prob / total).astype(jnp.bfloat16)
    mixed = jnp.einsum("shp,sphd->shd", weights, values_local, preferred_element_type=jnp.float32)
    mixed = mixed + self_weight.astype(jnp.float32)[:, :, None] * fresh_value.astype(jnp.float32)
    slot_out = mixed.reshape(slot_count, width_here).astype(jnp.bfloat16)
    slot_terms = jnp.dot(
        lax.all_gather(slot_out, ("rows", "role"), axis=0, tiled=True),
        out_proj,
        preferred_element_type=jnp.float32,
    )
    token_terms = jnp.take(slot_terms, placement, axis=0)
    head_sums = lax.psum_scatter(
        token_terms.astype(jnp.bfloat16), "tensor", scatter_dimension=0, tiled=True
    ).astype(jnp.float32)
    attended = (widened + head_sums).astype(jnp.bfloat16)
    attended_wide = attended.astype(jnp.float32)
    mix_squares = lax.psum(jnp.sum(attended_wide * attended_wide, axis=1), ("rows", "role"))
    mix_normed = (attended_wide * lax.rsqrt(mix_squares / D + 1e-05)[:, None] * mix_gain).astype(
        jnp.bfloat16
    )
    mix_terms = jnp.einsum(
        "rd,jde->jre",
        lax.all_gather(mix_normed, "tensor", axis=0, tiled=True),
        mix_proj,
        preferred_element_type=jnp.float32,
    )
    branches = lax.psum_scatter(
        mix_terms.astype(jnp.bfloat16), ("rows", "role"), scatter_dimension=1, tiled=True
    ).astype(jnp.float32)
    conv = (
        outer_taps[0][:, None, :] * branches
        + outer_taps[1][:, None, :] * outer_state[0].astype(jnp.float32)
        + outer_taps[2][:, None, :] * outer_state[1].astype(jnp.float32)
    )
    product = conv[0] * conv[2]
    filtered = (
        inner_taps[0] * product
        + inner_taps[1] * inner_state[0].astype(jnp.float32)
        + inner_taps[2] * inner_state[1].astype(jnp.float32)
    )
    gated = (conv[1] * filtered).astype(jnp.bfloat16)
    return (attended, gated)


def solution(mesh):
    return jax.shard_map(
        local,
        mesh=mesh,
        in_specs=(
            P(("groups", "tensor"), ("rows", "role")),
            P(("rows", "role")),
            P(None, ("rows", "role"), "tensor"),
            P(("groups", "rows", "role"), None, "tensor"),
            P(("groups", "rows", "role"), None, "tensor"),
            P(("groups", "rows", "role")),
            P("groups"),
            P("tensor", ("rows", "role")),
            P(("rows", "role")),
            P(None, ("rows", "role"), "tensor"),
            P(None, None, "tensor"),
            P(None, None, ("groups", "rows", "role"), "tensor"),
            P(None, "tensor"),
            P(None, ("groups", "rows", "role"), "tensor"),
        ),
        out_specs=(
            P(("groups", "tensor"), ("rows", "role")),
            P(("groups", "rows", "role"), "tensor"),
        ),
        check_vma=False,
    )
```

profile of v0, /device:TPU:0, one launch (start us, length us, event | category | flops | bytes accessed | tf_op | source)
XLA Modules:
  0.0 157.8 jit_solution(4077247140797194828)
XLA Ops:
  7.2 0.0 copy-start
  7.2 0.0 reduce-scatter.5.cloned.1.call-start
  7.2 0.7 compare_select_fusion.1
  8.0 0.7 compare_and_fusion.1
  8.6 0.9 fusion.15
  9.5 8.4 %psum.21 = f32[8]{0:T(128)S(1)} all-reduce(f32[8]{0:T(128)S(1)} %fusion.15), channel_id=1, replica_groups=mesh['groups'=2,'tensor'=4,'rows'=2,'role'=2] {'rows','role'}, use_global_device_ids=true, to_apply=%region_2.0 | all-reduce | flops 8 | bytes 64 | tf_op jit(solution)/shard_map/psum | solution.py:29
  17.9 0.8 fusion.17
  18.7 13.6 %all_gather.9 = bf16[32,2048]{1,0:T(8,128)(2,1)S(1)} all-gather(bf16[8,2048]{1,0:T(8,128)(2,1)S(1)} %fusion.17), channel_id=1, replica_groups=mesh['groups'=2,'tensor'=4,'rows'=2,'role'=2] {'tensor'}, dimensions={0}, use_global_device_ids=true | all-gather | bytes 163840 | tf_op jit(solution)/shard_map/all_gather | solution.py:33
  32.3 10.5 %convolution_bitcast_fusion = f32[3,32,2048]{2,1,0:T(8,128)S(1)} fusion(bf16[3,2048,2048]{2,1,0:T(8,128)(2,1)} %param.16, bf16[32,2048]{1,0:T(8,128)(2,1)S(1)} %all_gather.9), kind=kOutput, calls=%fused_computation.3 | convolution fusion | flops 805306368 | bytes 26083328 | tf_op jit(solution)/shard_map/rd,jde->jre/dot_general | solution.py:31
  42.9 18.9 %all-reduce.1 = bf16[3,32,2048]{2,1,0:T(8,128)(2,1)S(1)} all-reduce(f32[3,32,2048]{2,1,0:T(8,128)S(1)} %convolution_bitcast_fusion), channel_id=1, replica_groups=mesh['groups'=2,'tensor'=4,'rows'=2,'role'=2] {'rows','role'}, use_global_device_ids=true, to_apply=%region_3.0 | all-reduce | flops 196608 | bytes 1179648 | tf_op jit(solution)/shard_map/psum | solution.py:42
  61.7 0.3 copy.21
  62.1 0.7 scatter_custom_fusion
  62.8 0.1 compare_and_fusion
  62.9 0.7 gather_fusion
  63.6 0.1 fusion.9
  63.7 0.4 slice_reduce_fusion.1
  64.1 0.0 copy-done.8
  64.1 0.6 fusion.4
  64.7 0.0 copy-done.9
  64.7 0.1 iota_compare_fusion
  64.8 0.1 fusion.25
  64.9 0.1 select_reduce_fusion
  65.0 0.2 fusion.28
  65.2 0.1 fusion.31
  65.4 0.4 fusion.1
  65.7 0.1 fusion.30
  65.8 5.4 %all_gather.10 = bf16[32,2048]{1,0:T(8,128)(2,1)S(1)} all-gather(bf16[8,2048]{1,0:T(8,128)(2,1)S(1)} %bitcast.101), channel_id=1, replica_groups=mesh['groups'=2,'tensor'=4,'rows'=2,'role'=2] {'rows','role'}, dimensions={0}, use_global_device_ids=true | all-gather | bytes 163840 | tf_op jit(solution)/shard_map/all_gather | solution.py:73
  71.3 4.9 %fusion.38 = bf16[32,2048]{1,0:T(8,128)(2,1)S(1)} fusion(bf16[32,2048]{1,0:T(8,128)(2,1)S(1)} %all_gather.10, bf16[2048,2048]{1,0:T(8,128)(2,1)} %param.21), kind=kOutput, calls=%fused_computation.79 | convolution fusion | flops 268435456 | bytes 8650752 | tf_op jit(solution)/shard_map/dot_general | solution.py:72
  76.2 0.7 gather_fusion.1
  76.9 0.7 select_convert_fusion.1
  77.6 0.0 reduce-scatter.5.cloned.1.call-update
  77.6 0.0 reduce-scatter.7.cloned.1.call-start
  77.7 19.9 %reduce-scatter.5.cloned.1.call-done = bf16[8,2048]{1,0:T(8,128)(2,1)} async-done(((bf16[32,2048]{1,0:T(8,128)(2,1)}), bf16[8,2048]{1,0:T(8,128)(2,1)}) %reduce-scatter.5.cloned.1.call-update) | async-done | bytes 32784 | tf_op jit(solution)/shard_map/reduce_scatter | solution.py:78
  97.6 0.0 copy-done.1
  97.6 0.9 fusion.12
  98.5 5.7 %psum.23 = f32[8]{0:T(128)S(1)} all-reduce(f32[8]{0:T(128)S(1)} %get-tuple-element.4), channel_id=1, replica_groups=mesh['groups'=2,'tensor'=4,'rows'=2,'role'=2] {'rows','role'}, use_global_device_ids=true, to_apply=%region_8.9 | all-reduce | flops 8 | bytes 64 | tf_op jit(solution)/shard_map/psum | solution.py:83
  104.2 0.0 copy-done.7
  104.2 0.1 fusion.14
  104.2 13.5 %all_gather.11 = bf16[32,2048]{1,0:T(8,128)(2,1)S(1)} all-gather(bf16[8,2048]{1,0:T(8,128)(2,1)S(1)} %fusion.14), channel_id=1, replica_groups=mesh['groups'=2,'tensor'=4,'rows'=2,'role'=2] {'tensor'}, dimensions={0}, use_global_device_ids=true | all-gather | bytes 163840 | tf_op jit(solution)/shard_map/all_gather | solution.py:89
  117.8 10.5 %fusion = bf16[3,32,2048]{2,1,0:T(8,128)(2,1)S(1)} fusion(bf16[3,2048,2048]{2,1,0:T(8,128)(2,1)} %param.23, bf16[32,2048]{1,0:T(8,128)(2,1)S(1)} %all_gather.11), kind=kOutput, calls=%fused_computation.5 | convolution fusion | flops 805502976 | bytes 25690112 | tf_op jit(solution)/shard_map/rd,jde->jre/dot_general | solution.py:87
  128.3 0.3 copy.32
  128.7 1.0 copy.39
  129.7 0.0 reduce-scatter.7.cloned.1.call-update
  129.8 19.4 %reduce-scatter.7.cloned.1.call-done = bf16[8,6144]{1,0:T(8,128)(2,1)} async-done(((bf16[32,6144]{1,0:T(8,128)(2,1)}), bf16[8,6144]{1,0:T(8,128)(2,1)}) %reduce-scatter.7.cloned.1.call-update) | async-done | bytes 98320
  149.2 1.0 reshape.108
  150.2 0.0 copy-done.2
  150.2 0.1 fusion.7
  150.4 0.7 fusion.24
  (24 shorter events, 0.1 us)
Async XLA Ops:
  7.2 58.2 %copy-start = (bf16[8,32,2048]{2,1,0:T(8,128)(2,1)S(1)}, bf16[8,32,2048]{2,1,0:T(8,128)(2,1)}, u32[]{:S(2)}) copy-start(bf16[8,32,2048]{2,1,0:T(8,128)(2,1)} %param.18) | copy-start | bytes 3145732
  7.2 90.4 %reduce-scatter.5.cloned.1.call-start = ((), (), s32[]{:S(2)}) async-start(), calls=%async_computation.2 | async-start | bytes 163840 | tf_op jit(solution)/shard_map/reduce_scatter | solution.py:78
  32.3 31.7 %copy-start.8 = (bf16[8,32,2048]{2,1,0:T(8,128)(2,1)S(1)}, bf16[8,32,2048]{2,1,0:T(8,128)(2,1)}, u32[]{:S(2)}) copy-start(bf16[8,32,2048]{2,1,0:T(8,128)(2,1)} %param.17) | copy-start | bytes 3145732
  32.3 32.4 %copy-start.9 = (s32[8]{0:T(128)S(1)}, s32[8]{0:T(128)}, u32[]{:S(2)}) copy-start(s32[8]{0:T(128)} %param.19) | copy-start | bytes 100
  32.3 65.3 %copy-start.1 = (bf16[8,2048]{1,0:T(8,128)(2,1)S(1)}, bf16[8,2048]{1,0:T(8,128)(2,1)}, u32[]{:S(2)}) copy-start(bf16[8,2048]{1,0:T(8,128)(2,1)} %param.14) | copy-start | bytes 98308
  32.3 71.8 %copy-start.7 = (f32[2048]{0:T(1024)S(1)}, f32[2048]{0:T(1024)}, u32[]{:S(2)}) copy-start(f32[2048]{0:T(1024)} %param.22) | copy-start | bytes 24580
  77.6 71.6 %reduce-scatter.7.cloned.1.call-start = ((), (), s32[]{:S(2)}) async-start(), calls=%async_computation.3 | async-start | bytes 491520
  98.5 31.2 %copy-start.3 = (bf16[8,2048]{1,0:T(8,128)(2,1)}, bf16[8,2048]{1,0:T(8,128)(2,1)S(1)}, u32[]{:S(2)}) copy-start(bf16[8,2048]{1,0:T(8,128)(2,1)S(1)} %get-tuple-element.5) | copy-start | bytes 98308
  117.8 12.0 %copy-start.6 = (f32[3,2048]{1,0:T(4,128)S(1)}, f32[3,2048]{1,0:T(4,128)}, u32[]{:S(2)}) copy-start(f32[3,2048]{1,0:T(4,128)} %param.26) | copy-start | bytes 73732
  117.8 12.0 %copy-start.4 = (f32[3,3,2048]{2,1,0:T(4,128)S(1)}, f32[3,3,2048]{2,1,0:T(4,128)}, u32[]{:S(2)}) copy-start(f32[3,3,2048]{2,1,0:T(4,128)} %param.24) | copy-start | bytes 221188
  117.8 32.4 %copy-start.2 = (bf16[2,3,8,2048]{3,2,1,0:T(8,128)(2,1)S(1)}, bf16[2,3,8,2048]{3,2,1,0:T(8,128)(2,1)}, u32[]{:S(2)}) copy-start(bf16[2,3,8,2048]{3,2,1,0:T(8,128)(2,1)} %param.25) | copy-start | bytes 589828
  117.8 32.6 %copy-start.5 = (bf16[2,8,2048]{2,1,0:T(8,128)(2,1)S(1)}, bf16[2,8,2048]{2,1,0:T(8,128)(2,1)}, u32[]{:S(2)}) copy-start(bf16[2,8,2048]{2,1,0:T(8,128)(2,1)} %param.27) | copy-start | bytes 196612
Sparse Core Ops, SparseCore 0:
  77.7 19.8 reduce-scatter.4
  129.9 19.2 reduce-scatter.6
where the time goes:
time: 158 us
  blocking collectives  65.4 us (41%)
  waiting for transfers between devices  39.3 us (25%)
  matrix products  27 us (17%)
  between operations  14.3 us (9%)
  other arithmetic  6.88 us (4%)
  local copies, waits for them, and re-layouts  4.83 us (3%)
    reduce_scatter x1, waiting for transfers between devices, local(): lax.psum_scatter(token_terms.astype(jnp.bfloat16), 'tensor', scatter_dime...  19.9 us
    unnamed x3, waiting for transfers between devices  19.4 us
    psum x1, blocking collectives, local(): full = lax.psum(terms, ('rows', 'role'))  18.9 us
    all_gather x1, blocking collectives, local(): lax.all_gather(normed, 'tensor', axis=0, tiled=True)  13.6 us
    all_gather x1, blocking collectives, local(): lax.all_gather(mix_normed, 'tensor', axis=0, tiled=True)  13.5 us
    dot_general x1, matrix products, local(): jnp.einsum('rd,jde->jre', lax.all_gather(mix_normed, 'tensor', axis=0, ti...  10.5 us
    dot_general x1, matrix products, local(): jnp.einsum('rd,jde->jre', lax.all_gather(normed, 'tensor', axis=0, tiled=...  10.5 us
    psum x1, blocking collectives, local(): squares = lax.psum(jnp.sum(widened * widened, axis=1), ('rows', 'role'))  8.36 us
  transfers between devices with their start and end apart: 2, of which 2 were waited for; matrix products, arithmetic and copies ran while one was open for 0% of the time, Pallas kernels for 0%

commit v1 on v0

v1 whole, which is shorter than its diff:
```python
import functools
import math

import jax
import jax.numpy as jnp
from jax import lax
from jax.experimental import pallas as pl
from jax.experimental.pallas import tpu as pltpu
from jax.sharding import PartitionSpec as P

HEAD_DIM = 128
LANES = 128
EPS = 1e-05
VMEM = pl.BlockSpec(memory_space=pltpu.VMEM)
SMEM = pl.BlockSpec(memory_space=pltpu.SMEM)
ANY = pl.BlockSpec(memory_space=pl.ANY)
F32 = jnp.float32
BF16 = jnp.bfloat16
MIB = 2**20


def shape(dims, dtype):
    return jax.ShapeDtypeStruct(dims, dtype)


def call(kernel, outs, in_specs, scratch=(), limit=12, flops=0, moved=0, out_specs=None):
    return pl.pallas_call(
        kernel,
        out_shape=outs,
        in_specs=in_specs,
        out_specs=out_specs or [VMEM] * len(outs),
        scratch_shapes=scratch,
        compiler_params=pltpu.CompilerParams(vmem_limit_bytes=limit * MIB),
        cost_estimate=pl.CostEstimate(flops=flops, bytes_accessed=moved, transcendentals=0),
    )


def load_kernel(count, *refs):
    sources, _, targets, sems = refs[:count], refs[count], refs[count + 1 : 2 * count + 1], refs[-1]
    copies = [pltpu.make_async_copy(s, t, sems.at[i]) for i, (s, t) in enumerate(zip(sources, targets))]
    for copy in copies:
        copy.start()
    for copy in copies:
        copy.wait()


def load(arrays, after):
    moved = sum(a.size * a.dtype.itemsize for a in arrays)
    return call(
        functools.partial(load_kernel, len(arrays)),
        [pltpu.VMEM(a.shape, a.dtype) for a in arrays],
        [ANY] * (len(arrays) + 1),
        scratch=[pltpu.SemaphoreType.DMA((len(arrays),))],
        limit=2,
        flops=moved * 100,
        moved=moved,
    )(*[pltpu.with_memory_space_constraint(a, pltpu.HBM) for a in arrays], after)


def project(xp, gain, w_ref, own_ref, sends):
    block = own_ref.shape[0]
    width = w_ref.shape[2]
    squares = jnp.sum(xp * xp, axis=1, keepdims=True)
    gained = (xp * gain).astype(BF16)
    chunk = min(512, width)
    for j in range(3):
        for c in range(0, width, chunk):
            out = jnp.dot(gained, w_ref[j, :, c : c + chunk], preferred_element_type=F32)
            at = j * width + c
            own_ref[:, at : at + chunk] = out[:block]
            for e, send in enumerate(sends, 1):
                send[:, at : at + chunk] = out[e * block : (e + 1) * block].astype(BF16)
    lane = lax.broadcasted_iota(jnp.int32, (xp.shape[0], LANES), 1)
    high = squares.astype(BF16).astype(F32)
    rest = squares - high
    middle = rest.astype(BF16).astype(F32)
    low = rest - middle
    tail = jnp.where(lane == 0, high, jnp.where(lane == 1, middle, jnp.where(lane == 2, low, 0.0)))
    own_ref[:, 3 * width :] = tail[:block]
    for e, send in enumerate(sends, 1):
        send[:, 3 * width :] = tail[e * block : (e + 1) * block].astype(BF16)


def collect(features, own_ref, received):
    width = (own_ref.shape[1] - LANES) // 3
    total = own_ref[...]
    for ref in received:
        total = total + ref[...].astype(F32)
    squares = jnp.sum(total[:, 3 * width :], axis=1, keepdims=True)
    scale = lax.rsqrt(squares / features + EPS)
    return [total[:, j * width : (j + 1) * width] * scale for j in range(3)]


def first_kernel(n_t, n_g, *refs):
    parts, (index_ref, onehot_ref, gain_ref, w_ref) = refs[:n_t], refs[n_t : n_t + 4]
    x_ref, own_ref, *sends = refs[n_t + 4 :]
    rows = parts[0].shape[0]
    t = index_ref[0]
    for d in range(n_t):
        at = pl.multiple_of((t ^ d) * rows, rows)
        x_ref[pl.ds(at, rows), :] = parts[d][...].astype(F32)
    xp = jnp.dot(onehot_ref[...], x_ref[...].astype(BF16), preferred_element_type=F32)
    project(xp, gain_ref[...], w_ref, own_ref, sends)


def attend_kernel(n_g, features, *refs):
    own_ref, received = refs[0], refs[1:n_g]
    lengths_ref, keys_ref, values_ref, out_ref, rows_ref = refs[n_g:]
    slots, positions, width = keys_ref.shape
    heads = width // HEAD_DIM
    query, fresh_key, fresh_value = [
        a.astype(BF16).astype(F32) for a in collect(features, own_ref, received)
    ]
    mine = (
        lax.broadcasted_iota(jnp.int32, (heads, width), 1) // HEAD_DIM
        == lax.broadcasted_iota(jnp.int32, (heads, width), 0)
    )
    scale = 1.0 / math.sqrt(HEAD_DIM)
    position = lax.broadcasted_iota(jnp.int32, (heads, positions), 1)
    for s in range(slots):
        spread = jnp.where(mine, query[s : s + 1], 0.0)
        scores = scale * lax.dot_general(
            spread.astype(BF16), keys_ref[s], (((1,), (1,)), ((), ())), preferred_element_type=F32
        )
        own_score = scale * jnp.sum(spread * fresh_key[s : s + 1], axis=1, keepdims=True)
        live = position < lengths_ref[s]
        top = jnp.maximum(
            jnp.max(jnp.where(live, scores, -jnp.inf), axis=1, keepdims=True), own_score
        )
        probs = jnp.where(live, jnp.exp(scores - top), 0.0)
        self_prob = jnp.exp(own_score - top)
        total = jnp.sum(probs, axis=1, keepdims=True) + self_prob
        weights = (probs / total).astype(BF16)
        self_weight = (self_prob / total).astype(BF16).astype(F32)
        mixed = jnp.dot(weights, values_ref[s], preferred_element_type=F32)
        mixed = mixed + self_weight * fresh_value[s : s + 1]
        rows_ref[s : s + 1, :] = jnp.sum(jnp.where(mine, mixed, 0.0), axis=0, keepdims=True)
    out_ref[...] = rows_ref[...].astype(BF16)


def out_kernel(n_g, *refs):
    parts, (onehot_ref, w_ref) = refs[:n_g], refs[n_g : n_g + 2]
    own_ref, send_ref = refs[n_g + 2 :]
    gathered = jnp.concatenate([p[...].astype(F32) for p in parts], axis=0).astype(BF16)
    rows = jnp.dot(onehot_ref[...], gathered, preferred_element_type=F32).astype(BF16)
    width = w_ref.shape[1]
    chunk = min(512, width)
    for c in range(0, width, chunk):
        out = jnp.dot(rows, w_ref[:, c : c + chunk], preferred_element_type=F32)
        own_ref[:, c : c + chunk] = out
        send_ref[:, c : c + chunk] = out.astype(BF16)


def second_kernel(n_t, n_g, *refs):
    index_ref, x_ref, terms_ref = refs[:3]
    received = refs[3 : n_t + 2]
    gain_ref, w_ref, attended_ref, own_ref, *sends, scratch = refs[n_t + 2 :]
    rows, block = attended_ref.shape[0], own_ref.shape[0]
    total = terms_ref[...]
    for ref in received:
        total = total + ref[...].astype(F32)
    scratch[...] = (x_ref[...] + total).astype(BF16).astype(F32)
    at = pl.multiple_of(index_ref[0] * rows, rows)
    attended_ref[...] = scratch[pl.ds(at, rows), :].astype(BF16)
    g = index_ref[1]
    xp = jnp.concatenate(
        [scratch[pl.ds(pl.multiple_of((g ^ e) * block, block), block), :] for e in range(n_g)], axis=0
    )
    project(xp, gain_ref[...], w_ref, own_ref, sends)


def mixer_kernel(n_g, features, *refs):
    own_ref, received = refs[0], refs[1:n_g]
    outer_taps, outer_state, inner_taps, inner_state, out_ref = refs[n_g:]
    branches = collect(features, own_ref, received)
    conv = [
        outer_taps[0, j : j + 1] * branches[j]
        + outer_taps[1, j : j + 1] * outer_state[0, j].astype(F32)
        + outer_taps[2, j : j + 1] * outer_state[1, j].astype(F32)
        for j in range(3)
    ]
    filtered = (
        inner_taps[0:1] * (conv[0] * conv[2])
        + inner_taps[1:2] * inner_state[0].astype(F32)
        + inner_taps[2:3] * inner_state[1].astype(F32)
    )
    out_ref[...] = (conv[1] * filtered).astype(BF16)


def local(
    n_t,
    n_g,
    residual,
    attn_gain,
    attn_proj,
    cache_keys,
    cache_values,
    lengths,
    placement,
    out_proj,
    mix_gain,
    mix_proj,
    outer_taps,
    outer_state,
    inner_taps,
    inner_state,
):
    group = ("rows", "role")
    rows, depth = residual.shape
    slots = lengths.shape[0]
    batch = placement.shape[0]
    width = attn_proj.shape[2]
    features = depth * n_g
    t = lax.axis_index("tensor")
    g = lax.axis_index(group)
    index = jnp.stack([t, g]).astype(jnp.int32)

    def swap(x, axes, n, d):
        return lax.ppermute(x, axes, [(i, i ^ d) for i in range(n)])

    def products(n):
        return 2 * batch * depth * n

    parts = [residual] + [swap(residual, "tensor", n_t, d) for d in range(1, n_t)]
    place = jnp.arange(batch, dtype=jnp.int32)
    slot_of = ((g ^ (place // slots)) * slots + place % slots).astype(jnp.int32)
    to_slots = (slot_of[:, None] == placement[None, :]).astype(BF16)
    to_rows = (placement[:, None] == slot_of[None, :]).astype(BF16)

    (attn_w,) = load([attn_proj], index)
    payload = 3 * width + LANES
    branch_outs = [shape((slots, payload), F32)] + [shape((slots, payload), BF16)] * (n_g - 1)
    x, own, *sends = call(
        functools.partial(first_kernel, n_t, n_g),
        [shape((batch, depth), F32)] + branch_outs,
        [VMEM] * n_t + [SMEM] + [VMEM] * 3,
        flops=products(3 * width),
        moved=attn_proj.size * 2,
    )(*parts, index, to_slots, attn_gain.reshape(1, depth), attn_w)

    received = [swap(s, group, n_g, e) for e, s in enumerate(sends, 1)]
    keys, values, out_w = load([cache_keys, cache_values, out_proj], own)
    (slot_out,) = call(
        functools.partial(attend_kernel, n_g, features),
        [shape((slots, width), BF16)],
        [VMEM] * n_g + [SMEM, VMEM, VMEM],
        scratch=[pltpu.VMEM((slots, width), F32)],
        flops=4 * cache_keys.size,
        moved=cache_keys.size * 4,
    )(own, *received, lengths, keys, values)

    gathered = [slot_out] + [swap(slot_out, group, n_g, e) for e in range(1, n_g)]
    terms, send = call(
        functools.partial(out_kernel, n_g),
        [shape((batch, depth), F32), shape((batch, depth), BF16)],
        [VMEM] * (n_g + 2),
        flops=products(depth),
        moved=out_proj.size * 2,
    )(*gathered, to_rows, out_w)

    received = [swap(send, "tensor", n_t, d) for d in range(1, n_t)]
    (mix_w,) = load([mix_proj], terms)
    attended, own, *sends = call(
        functools.partial(second_kernel, n_t, n_g),
        [shape((rows, depth), BF16)] + branch_outs,
        [SMEM] + [VMEM] * (n_t + 3),
        scratch=[pltpu.VMEM((batch, depth), F32)],
        flops=products(3 * width),
        moved=mix_proj.size * 2,
    )(index, x, terms, *received, mix_gain.reshape(1, depth), mix_w)

    received = [swap(s, group, n_g, e) for e, s in enumerate(sends, 1)]
    (gated,) = call(
        functools.partial(mixer_kernel, n_g, features),
        [shape((slots, width), BF16)],
        [VMEM] * (n_g + 4),
        flops=slots * width * 40,
        moved=slots * width * 40,
    )(own, *received, outer_taps, outer_state, inner_taps, inner_state)
    return (attended, gated)


def solution(mesh):
    n_t = mesh.shape["tensor"]
    n_g = mesh.shape["rows"] * mesh.shape["role"]
    for n in (n_t, n_g):
        assert n & (n - 1) == 0, "axis size"
    return jax.shard_map(
        functools.partial(local, n_t, n_g),
        mesh=mesh,
        in_specs=(
            P(("groups", "tensor"), ("rows", "role")),
            P(("rows", "role")),
            P(None, ("rows", "role"), "tensor"),
            P(("groups", "rows", "role"), None, "tensor"),
            P(("groups", "rows", "role"), None, "tensor"),
            P(("groups", "rows", "role")),
            P("groups"),
            P("tensor", ("rows", "role")),
            P(("rows", "role")),
            P(None, ("rows", "role"), "tensor"),
            P(None, None, "tensor"),
            P(None, None, ("groups", "rows", "role"), "tensor"),
            P(None, "tensor"),
            P(None, ("groups", "rows", "role"), "tensor"),
        ),
        out_specs=(
            P(("groups", "tensor"), ("rows", "role")),
            P(("groups", "rows", "role"), "tensor"),
        ),
        check_vma=False,
    )
```

time: 158 us -> 64.8 us (0.41)
  blocking collectives: 65.4 us -> 0 us
  Pallas kernels: 0 us -> 37.4 us
  waiting for transfers between devices: 39.3 us -> 10.3 us
  matrix products: 27 us -> 0 us
  starting transfers between devices: 0.08 us -> 15.9 us
  between operations: 14.3 us -> 0.8 us
  other arithmetic: 6.88 us -> 0.16 us
  local copies, waits for them, and re-layouts: 4.83 us -> 0.05 us
    pallas_call x0 -> x8, Pallas kernels: none -> 37.4 us  [the longest x3 20.4 us: load(): call(functools.partial(load_kernel, len(arrays)), [pltpu.VMEM(a.shape, a....]
    psum x3 -> x0, blocking collectives: 32.9 us -> none  [the longest x1 18.9 us: local(): full = lax.psum(terms, ('rows', 'role'))]
    all_gather x3 -> x0, blocking collectives: 32.5 us -> none  [the longest x1 13.6 us: local(): lax.all_gather(normed, 'tensor', axis=0, tiled=True)]
    dot_general x5 -> x0, matrix products: 27 us -> none  [the longest x1 10.5 us: local(): jnp.einsum('rd,jde->jre', lax.all_gather(mix_normed, 'tensor', axis=0, ti...]
    reduce_scatter x1 -> x0, waiting for transfers between devices: 19.9 us -> none  [local(): lax.psum_scatter(token_terms.astype(jnp.bfloat16), 'tensor', scatter_dime...]
    unnamed x3 -> x0, waiting for transfers between devices: 19.4 us -> none
    ppermute x0 -> x15, starting transfers between devices: none -> 15.9 us  [swap(): return lax.ppermute(x, axes, [(i, i ^ d) for i in range(n)])]
    ppermute x0 -> x15, waiting for transfers between devices: none -> 10.3 us  [swap(): return lax.ppermute(x, axes, [(i, i ^ d) for i in range(n)])]
  transfers between devices with their start and end apart: 2 -> 15, of which waited for: 2 -> 6; matrix products, arithmetic and copies ran while one was open for 0% -> 0% of each run, Pallas kernels for 0% -> 32%
where the time goes in v1:
time: 64.8 us; the launch traced here: 64.6 us
  Pallas kernels  37.4 us (58%)
  starting transfers between devices  15.9 us (25%)
  waiting for transfers between devices  10.3 us (16%)
  between operations  0.8 us (1%)
    pallas_call x3, Pallas kernels, load(): call(functools.partial(load_kernel, len(arrays)), [pltpu.VMEM(a.shape, a....  20.4 us
    ppermute x15, starting transfers between devices, swap(): return lax.ppermute(x, axes, [(i, i ^ d) for i in range(n)])  15.9 us
    ppermute x15, waiting for transfers between devices, swap(): return lax.ppermute(x, axes, [(i, i ^ d) for i in range(n)])  10.3 us
    pallas_call x1, Pallas kernels, local(): call(functools.partial(second_kernel, n_t, n_g), [shape((rows, depth), BF...  5.59 us
    pallas_call x1, Pallas kernels, local(): call(functools.partial(first_kernel, n_t, n_g), [shape((batch, depth), F3...  5.12 us
    pallas_call x1, Pallas kernels, local(): call(functools.partial(attend_kernel, n_g, features), [shape((slots, widt...  3.87 us
    pallas_call x1, Pallas kernels, local(): call(functools.partial(out_kernel, n_g), [shape((batch, depth), F32), sha...  1.65 us
  transfers between devices with their start and end apart: 15, of which 6 were waited for; matrix products, arithmetic and copies ran while one was open for 0% of the time, Pallas kernels for 32%

profile of v1, /device:TPU:0, one launch (start us, length us, event | category | flops | bytes accessed | tf_op | source)
XLA Modules:
  0.0 64.6 jit_solution(10631735581679706982)
XLA Ops:
  0.6 4.1 %collective-permute-start.1 = (bf16[8,2048]{1,0:T(8,128)(2,1)}, bf16[8,2048]{1,0:T(8,128)(2,1)S(1)}, u32[]{:S(2)}, u32[]{:S(2)}) collective-permute-start(bf16[8,2048]{1,0:T(8,128)(2,1)} %refs_0_.5), channel_id=1, source_target_pairs={{0,8},{4,12},{8,0},{12,4},{1,9},{5,13},{9,1},{13,5},{2,10},{6,14},... | collective-permute-start | bytes 98312 | tf_op jit(solution)/shard_map/ppermute | solution.py:219
  4.8 1.6 %collective-permute-start = (bf16[8,2048]{1,0:T(8,128)(2,1)}, bf16[8,2048]{1,0:T(8,128)(2,1)S(1)}, u32[]{:S(2)}, u32[]{:S(2)}) collective-permute-start(bf16[8,2048]{1,0:T(8,128)(2,1)} %refs_0_.5), channel_id=1, source_target_pairs={{0,4},{4,0},{8,12},{12,8},{1,5},{5,1},{9,13},{13,9},{2,6},{6,2},{1... | collective-permute-start | bytes 98312 | tf_op jit(solution)/shard_map/ppermute | solution.py:219
  6.3 0.0 collective-permute-start.2
  6.3 0.1 pad_add_fusion.refs_1_.refs_4_.refs_0_
  6.4 8.2 %shard_map.149.refs_7_ = bf16[3,2048,2048]{2,1,0:T(8,128)(2,1)S(1)} custom-call(bf16[3,2048,2048]{2,1,0:T(8,128)(2,1)} %refs_0_.4, s32[2]{0:T(128)S(1)} %pad_add_fusion.refs_1_.refs_4_.refs_0_), custom_call_target="tpu_custom_call" | custom-call | flops 2516582400 | bytes 25165824 | tf_op jit(solution)/shard_map/pallas_call | solution.py:49
  14.6 0.0 copy-done.8
  14.6 0.0 copy-start.7
  14.6 0.1 compare_convert_fusion
  14.7 0.0 collective-permute-done.1.refs_2_
  14.7 0.0 collective-permute-done.refs_1_
  14.7 0.0 collective-permute-done.2.refs_3_
  14.7 0.0 copy-done.3
  14.8 5.1 %shard_map.150 = (f32[32,2048]{1,0:T(8,128)S(1)}, f32[8,6272]{1,0:T(8,128)S(1)}, bf16[8,6272]{1,0:T(8,128)(2,1)S(1)}, bf16[8,6272]{1,0:T(8,128)(2,1)S(1)}, bf16[8,6272]{1,0:T(8,128)(2,1)S(1)}) custom-call(bf16[8,2048]{1,0:T(8,128)(2,1)S(1)} %copy-done.3, bf16[8,2048]{1,0:T(8,128)(2,1)S(1)} %collective-permute-done.refs_1_, ...), custom_call_target="tpu_custom_call" | custom-call | flops 805306368 | bytes 25165824 | tf_op jit(solution)/shard_map/pallas_call | solution.py:233
  19.9 0.0 collective-permute-start.3
  19.9 1.8 %collective-permute-start.4 = (bf16[8,6272]{1,0:T(8,128)(2,1)S(1)}, bf16[8,6272]{1,0:T(8,128)(2,1)S(1)}, u32[]{:S(2)}, u32[]{:S(2)}) collective-permute-start(bf16[8,6272]{1,0:T(8,128)(2,1)S(1)} %get-tuple-element.20), channel_id=1, source_target_pairs={{0,2},{1,3},{2,0},{3,1},{4,6},{5,7},{6,4},{7,5},{8,10},{9,11},{10,... | collective-permute-start | bytes 301064 | tf_op jit(solution)/shard_map/ppermute | solution.py:219
  21.7 0.1 collective-permute-start.5
  21.8 4.1 %shard_map.151 = (bf16[8,32,2048]{2,1,0:T(8,128)(2,1)S(1)}, bf16[8,32,2048]{2,1,0:T(8,128)(2,1)S(1)}, bf16[2048,2048]{1,0:T(8,128)(2,1)S(1)}) custom-call(bf16[8,32,2048]{2,1,0:T(8,128)(2,1)} %refs_0_.6, bf16[8,32,2048]{2,1,0:T(8,128)(2,1)} %refs_1_.1, bf16[2048,2048]{1,0:T(8,128)(2,1)} %refs_2_.1, f32[8,6272]{1,0:T(8,128)S(1)} %get-tuple-element.18.refs_3_.refs_0_), custom_call_target="tpu_custom_call" | custom-call | flops 1048576000 | bytes 10485760 | tf_op jit(solution)/shard_map/pallas_call | solution.py:49
  25.9 0.0 collective-permute-done.3.refs_1_
  25.9 0.0 collective-permute-done.4.refs_2_
  25.9 1.0 %collective-permute-done.5.refs_3_ = bf16[8,6272]{1,0:T(8,128)(2,1)S(1)} collective-permute-done((bf16[8,6272]{1,0:T(8,128)(2,1)S(1)}, bf16[8,6272]{1,0:T(8,128)(2,1)S(1)}, u32[]{:S(2)}, u32[]{:S(2)}) %collective-permute-start.5) | collective-permute-done | bytes 100384 | tf_op jit(solution)/shard_map/ppermute | solution.py:219
  26.9 3.9 %shard_map.152.refs_0_ = bf16[8,2048]{1,0:T(8,128)(2,1)S(1)} custom-call(f32[8,6272]{1,0:T(8,128)S(1)} %get-tuple-element.18.refs_3_.refs_0_, bf16[8,6272]{1,0:T(8,128)(2,1)S(1)} %collective-permute-done.3.refs_1_, bf16[8,6272]{1,0:T(8,128)(2,1)S(1)} %collective-permute-done.4.refs_2_, bf16[8,6272]{1,0:T(8,128)(2,1)S(1)} %collective-permute-done.5.refs_3_, ...), custom_call_target="tpu_custom_call" | custom-call | flops 2097152 | bytes 2097152 | tf_op jit(solution)/shard_map/pallas_call | solution.py:243
  30.7 1.7 %collective-permute-start.8 = (bf16[8,2048]{1,0:T(8,128)(2,1)S(1)}, bf16[8,2048]{1,0:T(8,128)(2,1)S(1)}, u32[]{:S(2)}, u32[]{:S(2)}) collective-permute-start(bf16[8,2048]{1,0:T(8,128)(2,1)S(1)} %shard_map.152.refs_0_), channel_id=1, source_target_pairs={{0,3},{1,2},{2,1},{3,0},{4,7},{5,6},{6,5},{7,4},{8,11},{9,10},{10,... | collective-permute-start | bytes 98312 | tf_op jit(solution)/shard_map/ppermute | solution.py:219
  32.4 0.3 collective-permute-start.7
  32.7 0.0 collective-permute-start.6
  32.7 1.4 %collective-permute-done.8.refs_3_ = bf16[8,2048]{1,0:T(8,128)(2,1)S(1)} collective-permute-done((bf16[8,2048]{1,0:T(8,128)(2,1)S(1)}, bf16[8,2048]{1,0:T(8,128)(2,1)S(1)}, u32[]{:S(2)}, u32[]{:S(2)}) %collective-permute-start.8) | collective-permute-done | bytes 32800 | tf_op jit(solution)/shard_map/ppermute | solution.py:219
  34.1 2.2 %collective-permute-done.7.refs_2_ = bf16[8,2048]{1,0:T(8,128)(2,1)S(1)} collective-permute-done((bf16[8,2048]{1,0:T(8,128)(2,1)S(1)}, bf16[8,2048]{1,0:T(8,128)(2,1)S(1)}, u32[]{:S(2)}, u32[]{:S(2)}) %collective-permute-start.7) | collective-permute-done | bytes 32800 | tf_op jit(solution)/shard_map/ppermute | solution.py:219
  36.3 0.0 collective-permute-done.6.refs_1_
  36.3 1.6 %shard_map.153 = (f32[32,2048]{1,0:T(8,128)S(1)}, bf16[32,2048]{1,0:T(8,128)(2,1)S(1)}) custom-call(bf16[8,2048]{1,0:T(8,128)(2,1)S(1)} %shard_map.152.refs_0_, bf16[8,2048]{1,0:T(8,128)(2,1)S(1)} %collective-permute-done.6.refs_1_, bf16[8,2048]{1,0:T(8,128)(2,1)S(1)} %collective-permute-done.7.refs_2_, bf16[8,2048]{1,0:T(8,128)(2,1)S(1)} %collective-permute-done.8.refs_3_, ...), custom_call_target="tpu_custom_call" | custom-call | flops 268435456 | bytes 8388608 | tf_op jit(solution)/shard_map/pallas_call | solution.py:253
  38.0 3.6 %collective-permute-start.11 = (bf16[32,2048]{1,0:T(8,128)(2,1)S(1)}, bf16[32,2048]{1,0:T(8,128)(2,1)S(1)}, u32[]{:S(2)}, u32[]{:S(2)}) collective-permute-start(bf16[32,2048]{1,0:T(8,128)(2,1)S(1)} %get-tuple-element.26), channel_id=1, source_target_pairs={{0,12},{4,8},{8,4},{12,0},{1,13},{5,9},{9,5},{13,1},{2,14},{6,10},... | collective-permute-start | bytes 393224 | tf_op jit(solution)/shard_map/ppermute | solution.py:219
  41.6 0.0 collective-permute-start.10
  41.6 0.8 %collective-permute-start.9 = (bf16[32,2048]{1,0:T(8,128)(2,1)S(1)}, bf16[32,2048]{1,0:T(8,128)(2,1)S(1)}, u32[]{:S(2)}, u32[]{:S(2)}) collective-permute-start(bf16[32,2048]{1,0:T(8,128)(2,1)S(1)} %get-tuple-element.26), channel_id=1, source_target_pairs={{0,4},{4,0},{8,12},{12,8},{1,5},{5,1},{9,13},{13,9},{2,6},{6,2},{1... | collective-permute-start | bytes 393224 | tf_op jit(solution)/shard_map/ppermute | solution.py:219
  42.4 8.2 %shard_map.154.refs_7_ = bf16[3,2048,2048]{2,1,0:T(8,128)(2,1)S(1)} custom-call(bf16[3,2048,2048]{2,1,0:T(8,128)(2,1)} %refs_0_.7, f32[32,2048]{1,0:T(8,128)S(1)} %get-tuple-element.25.refs_1_.refs_2_), custom_call_target="tpu_custom_call" | custom-call | flops 2516582400 | bytes 25165824 | tf_op jit(solution)/shard_map/pallas_call | solution.py:49
  50.6 0.0 copy-start
  50.6 0.0 copy-start.1
  50.6 0.0 copy-start.2
  50.6 0.0 copy-start.4
  50.6 0.0 collective-permute-done.11.refs_5_
  50.6 0.6 %collective-permute-done.10.refs_4_ = bf16[32,2048]{1,0:T(8,128)(2,1)S(1)} collective-permute-done((bf16[32,2048]{1,0:T(8,128)(2,1)S(1)}, bf16[32,2048]{1,0:T(8,128)(2,1)S(1)}, u32[]{:S(2)}, u32[]{:S(2)}) %collective-permute-start.10) | collective-permute-done | bytes 131104 | tf_op jit(solution)/shard_map/ppermute | solution.py:219
  51.3 0.0 collective-permute-done.9.refs_3_
  51.3 5.6 %shard_map.155 = (bf16[8,2048]{1,0:T(8,128)(2,1)}, f32[8,6272]{1,0:T(8,128)S(1)}, bf16[8,6272]{1,0:T(8,128)(2,1)S(1)}, bf16[8,6272]{1,0:T(8,128)(2,1)S(1)}, bf16[8,6272]{1,0:T(8,128)(2,1)S(1)}) custom-call(s32[2]{0:T(128)S(1)} %pad_add_fusion.refs_1_.refs_4_.refs_0_, f32[32,2048]{1,0:T(8,128)S(1)} %get-tuple-element.17.refs_1_, ...), custom_call_target="tpu_custom_call" | custom-call | flops 805306368 | bytes 25165824 | tf_op jit(solution)/shard_map/pallas_call | solution.py:263
  56.9 0.0 collective-permute-start.12
  56.9 0.8 %collective-permute-start.13 = (bf16[8,6272]{1,0:T(8,128)(2,1)S(1)}, bf16[8,6272]{1,0:T(8,128)(2,1)S(1)}, u32[]{:S(2)}, u32[]{:S(2)}) collective-permute-start(bf16[8,6272]{1,0:T(8,128)(2,1)S(1)} %get-tuple-element.30), channel_id=1, source_target_pairs={{0,2},{1,3},{2,0},{3,1},{4,6},{5,7},{6,4},{7,5},{8,10},{9,11},{10,... | collective-permute-start | bytes 301064 | tf_op jit(solution)/shard_map/ppermute | solution.py:219
  57.6 1.1 %collective-permute-start.14 = (bf16[8,6272]{1,0:T(8,128)(2,1)S(1)}, bf16[8,6272]{1,0:T(8,128)(2,1)S(1)}, u32[]{:S(2)}, u32[]{:S(2)}) collective-permute-start(bf16[8,6272]{1,0:T(8,128)(2,1)S(1)} %get-tuple-element.31), channel_id=1, source_target_pairs={{0,3},{1,2},{2,1},{3,0},{4,7},{5,6},{6,5},{7,4},{8,11},{9,10},{10,... | collective-permute-start | bytes 301064 | tf_op jit(solution)/shard_map/ppermute | solution.py:219
  58.7 0.0 collective-permute-done.12.refs_1_
  58.7 3.9 %collective-permute-done.13.refs_2_ = bf16[8,6272]{1,0:T(8,128)(2,1)S(1)} collective-permute-done((bf16[8,6272]{1,0:T(8,128)(2,1)S(1)}, bf16[8,6272]{1,0:T(8,128)(2,1)S(1)}, u32[]{:S(2)}, u32[]{:S(2)}) %collective-permute-start.13) | collective-permute-done | bytes 100384 | tf_op jit(solution)/shard_map/ppermute | solution.py:219
  62.6 1.2 %collective-permute-done.14.refs_3_ = bf16[8,6272]{1,0:T(8,128)(2,1)S(1)} collective-permute-done((bf16[8,6272]{1,0:T(8,128)(2,1)S(1)}, bf16[8,6272]{1,0:T(8,128)(2,1)S(1)}, u32[]{:S(2)}, u32[]{:S(2)}) %collective-permute-start.14) | collective-permute-done | bytes 100384 | tf_op jit(solution)/shard_map/ppermute | solution.py:219
  63.8 0.0 copy-done.4
  63.8 0.8 %shard_map.156 = bf16[8,2048]{1,0:T(8,128)(2,1)} custom-call(f32[8,6272]{1,0:T(8,128)S(1)} %get-tuple-element.28.refs_0_, bf16[8,6272]{1,0:T(8,128)(2,1)S(1)} %collective-permute-done.12.refs_1_, bf16[8,6272]{1,0:T(8,128)(2,1)S(1)} %collective-permute-done.13.refs_2_, bf16[8,6272]{1,0:T(8,128)(2,1)S(1)} %collective-permute-done.14.refs_3_, ...), custom_call_target="tpu_custom_call" | custom-call | flops 655360 | bytes 655360 | tf_op jit(solution)/shard_map/pallas_call | solution.py:273
  (11 shorter events, 0.0 us)
Async XLA Ops:
  0.6 14.1 %collective-permute-start.1 = (bf16[8,2048]{1,0:T(8,128)(2,1)}, bf16[8,2048]{1,0:T(8,128)(2,1)S(1)}, u32[]{:S(2)}, u32[]{:S(2)}) collective-permute-start(bf16[8,2048]{1,0:T(8,128)(2,1)} %refs_0_.5), channel_id=1, source_target_pairs={{0,8},{4,12},{8,0},{12,4},{1,9},{5,13},{9,1},{13,5},{2,10},{6,14},... | collective-permute-start | bytes 98312 | tf_op jit(solution)/shard_map/ppermute | solution.py:219
  4.8 10.0 %collective-permute-start = (bf16[8,2048]{1,0:T(8,128)(2,1)}, bf16[8,2048]{1,0:T(8,128)(2,1)S(1)}, u32[]{:S(2)}, u32[]{:S(2)}) collective-permute-start(bf16[8,2048]{1,0:T(8,128)(2,1)} %refs_0_.5), channel_id=1, source_target_pairs={{0,4},{4,0},{8,12},{12,8},{1,5},{5,1},{9,13},{13,9},{2,6},{6,2},{1... | collective-permute-start | bytes 98312 | tf_op jit(solution)/shard_map/ppermute | solution.py:219
  6.3 8.4 %collective-permute-start.2 = (bf16[8,2048]{1,0:T(8,128)(2,1)}, bf16[8,2048]{1,0:T(8,128)(2,1)S(1)}, u32[]{:S(2)}, u32[]{:S(2)}) collective-permute-start(bf16[8,2048]{1,0:T(8,128)(2,1)} %refs_0_.5), channel_id=1, source_target_pairs={{0,12},{4,8},{8,4},{12,0},{1,13},{5,9},{9,5},{13,1},{2,14},{6,10},... | collective-permute-start | bytes 98312 | tf_op jit(solution)/shard_map/ppermute | solution.py:219
  6.4 8.2 %copy-start.8 = (s32[32]{0:T(128)S(1)}, s32[32]{0:T(128)}, u32[]{:S(2)}) copy-start(s32[32]{0:T(128)} %param.20) | copy-start | bytes 388
  6.4 8.3 %copy-start.3 = (bf16[8,2048]{1,0:T(8,128)(2,1)S(1)}, bf16[8,2048]{1,0:T(8,128)(2,1)}, u32[]{:S(2)}) copy-start(bf16[8,2048]{1,0:T(8,128)(2,1)} %refs_0_.5) | copy-start | bytes 98308
  6.4 8.3 %copy-start.5 = (f32[2048]{0:T(1024)S(1)}, f32[2048]{0:T(1024)}, u32[]{:S(2)}) copy-start(f32[2048]{0:T(1024)} %param.15) | copy-start | bytes 24580
  14.6 12.2 %copy-start.7 = (s32[8]{0:T(128)S(1)}, s32[8]{0:T(128)}, u32[]{:S(2)}) copy-start(s32[8]{0:T(128)} %refs_4_.2) | copy-start | bytes 100
  19.9 6.0 %collective-permute-start.3 = (bf16[8,6272]{1,0:T(8,128)(2,1)S(1)}, bf16[8,6272]{1,0:T(8,128)(2,1)S(1)}, u32[]{:S(2)}, u32[]{:S(2)}) collective-permute-start(bf16[8,6272]{1,0:T(8,128)(2,1)S(1)} %get-tuple-element.19), channel_id=1, source_target_pairs={{0,1},{1,0},{2,3},{3,2},{4,5},{5,4},{6,7},{7,6},{8,9},{9,8},{10,11... | collective-permute-start | bytes 301064 | tf_op jit(solution)/shard_map/ppermute | solution.py:219
  19.9 5.9 %collective-permute-start.4 = (bf16[8,6272]{1,0:T(8,128)(2,1)S(1)}, bf16[8,6272]{1,0:T(8,128)(2,1)S(1)}, u32[]{:S(2)}, u32[]{:S(2)}) collective-permute-start(bf16[8,6272]{1,0:T(8,128)(2,1)S(1)} %get-tuple-element.20), channel_id=1, source_target_pairs={{0,2},{1,3},{2,0},{3,1},{4,6},{5,7},{6,4},{7,5},{8,10},{9,11},{10,... | collective-permute-start | bytes 301064 | tf_op jit(solution)/shard_map/ppermute | solution.py:219
  21.7 5.1 %collective-permute-start.5 = (bf16[8,6272]{1,0:T(8,128)(2,1)S(1)}, bf16[8,6272]{1,0:T(8,128)(2,1)S(1)}, u32[]{:S(2)}, u32[]{:S(2)}) collective-permute-start(bf16[8,6272]{1,0:T(8,128)(2,1)S(1)} %get-tuple-element.21), channel_id=1, source_target_pairs={{0,3},{1,2},{2,1},{3,0},{4,7},{5,6},{6,5},{7,4},{8,11},{9,10},{10,... | collective-permute-start | bytes 301064 | tf_op jit(solution)/shard_map/ppermute | solution.py:219
  30.7 3.4 %collective-permute-start.8 = (bf16[8,2048]{1,0:T(8,128)(2,1)S(1)}, bf16[8,2048]{1,0:T(8,128)(2,1)S(1)}, u32[]{:S(2)}, u32[]{:S(2)}) collective-permute-start(bf16[8,2048]{1,0:T(8,128)(2,1)S(1)} %shard_map.152.refs_0_), channel_id=1, source_target_pairs={{0,3},{1,2},{2,1},{3,0},{4,7},{5,6},{6,5},{7,4},{8,11},{9,10},{10,... | collective-permute-start | bytes 98312 | tf_op jit(solution)/shard_map/ppermute | solution.py:219
  32.4 3.9 %collective-permute-start.7 = (bf16[8,2048]{1,0:T(8,128)(2,1)S(1)}, bf16[8,2048]{1,0:T(8,128)(2,1)S(1)}, u32[]{:S(2)}, u32[]{:S(2)}) collective-permute-start(bf16[8,2048]{1,0:T(8,128)(2,1)S(1)} %shard_map.152.refs_0_), channel_id=1, source_target_pairs={{0,2},{1,3},{2,0},{3,1},{4,6},{5,7},{6,4},{7,5},{8,10},{9,11},{10,... | collective-permute-start | bytes 98312 | tf_op jit(solution)/shard_map/ppermute | solution.py:219
  32.7 3.6 %collective-permute-start.6 = (bf16[8,2048]{1,0:T(8,128)(2,1)S(1)}, bf16[8,2048]{1,0:T(8,128)(2,1)S(1)}, u32[]{:S(2)}, u32[]{:S(2)}) collective-permute-start(bf16[8,2048]{1,0:T(8,128)(2,1)S(1)} %shard_map.152.refs_0_), channel_id=1, source_target_pairs={{0,1},{1,0},{2,3},{3,2},{4,5},{5,4},{6,7},{7,6},{8,9},{9,8},{10,11... | collective-permute-start | bytes 98312 | tf_op jit(solution)/shard_map/ppermute | solution.py:219
  38.0 12.6 %collective-permute-start.11 = (bf16[32,2048]{1,0:T(8,128)(2,1)S(1)}, bf16[32,2048]{1,0:T(8,128)(2,1)S(1)}, u32[]{:S(2)}, u32[]{:S(2)}) collective-permute-start(bf16[32,2048]{1,0:T(8,128)(2,1)S(1)} %get-tuple-element.26), channel_id=1, source_target_pairs={{0,12},{4,8},{8,4},{12,0},{1,13},{5,9},{9,5},{13,1},{2,14},{6,10},... | collective-permute-start | bytes 393224 | tf_op jit(solution)/shard_map/ppermute | solution.py:219
  41.6 9.7 %collective-permute-start.10 = (bf16[32,2048]{1,0:T(8,128)(2,1)S(1)}, bf16[32,2048]{1,0:T(8,128)(2,1)S(1)}, u32[]{:S(2)}, u32[]{:S(2)}) collective-permute-start(bf16[32,2048]{1,0:T(8,128)(2,1)S(1)} %get-tuple-element.26), channel_id=1, source_target_pairs={{0,8},{4,12},{8,0},{12,4},{1,9},{5,13},{9,1},{13,5},{2,10},{6,14},... | collective-permute-start | bytes 393224 | tf_op jit(solution)/shard_map/ppermute | solution.py:219
  41.6 9.7 %collective-permute-start.9 = (bf16[32,2048]{1,0:T(8,128)(2,1)S(1)}, bf16[32,2048]{1,0:T(8,128)(2,1)S(1)}, u32[]{:S(2)}, u32[]{:S(2)}) collective-permute-start(bf16[32,2048]{1,0:T(8,128)(2,1)S(1)} %get-tuple-element.26), channel_id=1, source_target_pairs={{0,4},{4,0},{8,12},{12,8},{1,5},{5,1},{9,13},{13,9},{2,6},{6,2},{1... | collective-permute-start | bytes 393224 | tf_op jit(solution)/shard_map/ppermute | solution.py:219
  42.4 8.9 %copy-start.6 = (f32[2048]{0:T(1024)S(1)}, f32[2048]{0:T(1024)}, u32[]{:S(2)}) copy-start(f32[2048]{0:T(1024)} %param.22) | copy-start | bytes 24580
  50.6 13.2 %copy-start = (bf16[2,3,8,2048]{3,2,1,0:T(8,128)(2,1)S(1)}, bf16[2,3,8,2048]{3,2,1,0:T(8,128)(2,1)}, u32[]{:S(2)}) copy-start(bf16[2,3,8,2048]{3,2,1,0:T(8,128)(2,1)} %refs_5_.1) | copy-start | bytes 589828
  50.6 13.2 %copy-start.1 = (f32[3,3,2048]{2,1,0:T(4,128)S(1)}, f32[3,3,2048]{2,1,0:T(4,128)}, u32[]{:S(2)}) copy-start(f32[3,3,2048]{2,1,0:T(4,128)} %refs_4_.3) | copy-start | bytes 221188
  50.6 13.2 %copy-start.2 = (bf16[2,8,2048]{2,1,0:T(8,128)(2,1)S(1)}, bf16[2,8,2048]{2,1,0:T(8,128)(2,1)}, u32[]{:S(2)}) copy-start(bf16[2,8,2048]{2,1,0:T(8,128)(2,1)} %refs_7_.1) | copy-start | bytes 196612
  50.6 13.2 %copy-start.4 = (f32[3,2048]{1,0:T(4,128)S(1)}, f32[3,2048]{1,0:T(4,128)}, u32[]{:S(2)}) copy-start(f32[3,2048]{1,0:T(4,128)} %refs_6_.1) | copy-start | bytes 73732
  56.9 1.9 %collective-permute-start.12 = (bf16[8,6272]{1,0:T(8,128)(2,1)S(1)}, bf16[8,6272]{1,0:T(8,128)(2,1)S(1)}, u32[]{:S(2)}, u32[]{:S(2)}) collective-permute-start(bf16[8,6272]{1,0:T(8,128)(2,1)S(1)} %get-tuple-element.29), channel_id=1, source_target_pairs={{0,1},{1,0},{2,3},{3,2},{4,5},{5,4},{6,7},{7,6},{8,9},{9,8},{10,11... | collective-permute-start | bytes 301064 | tf_op jit(solution)/shard_map/ppermute | solution.py:219
  56.9 5.7 %collective-permute-start.13 = (bf16[8,6272]{1,0:T(8,128)(2,1)S(1)}, bf16[8,6272]{1,0:T(8,128)(2,1)S(1)}, u32[]{:S(2)}, u32[]{:S(2)}) collective-permute-start(bf16[8,6272]{1,0:T(8,128)(2,1)S(1)} %get-tuple-element.30), channel_id=1, source_target_pairs={{0,2},{1,3},{2,0},{3,1},{4,6},{5,7},{6,4},{7,5},{8,10},{9,11},{10,... | collective-permute-start | bytes 301064 | tf_op jit(solution)/shard_map/ppermute | solution.py:219
  57.6 6.2 %collective-permute-start.14 = (bf16[8,6272]{1,0:T(8,128)(2,1)S(1)}, bf16[8,6272]{1,0:T(8,128)(2,1)S(1)}, u32[]{:S(2)}, u32[]{:S(2)}) collective-permute-start(bf16[8,6272]{1,0:T(8,128)(2,1)S(1)} %get-tuple-element.31), channel_id=1, source_target_pairs={{0,3},{1,2},{2,1},{3,0},{4,7},{5,6},{6,5},{7,4},{8,11},{9,10},{10,... | collective-permute-start | bytes 301064 | tf_op jit(solution)/shard_map/ppermute | solution.py:219

commit v2 on v0

v2 whole, which is shorter than its diff:
```python
import functools
import math

import jax
import jax.numpy as jnp
from jax import lax
from jax.experimental import pallas as pl
from jax.experimental.pallas import tpu as pltpu
from jax.sharding import PartitionSpec as P

HEAD_DIM = 128
LANES = 128
EPS = 1e-05
GROUP = ("rows", "role")
VMEM = pl.BlockSpec(memory_space=pltpu.VMEM)
SMEM = pl.BlockSpec(memory_space=pltpu.SMEM)
ANY = pl.BlockSpec(memory_space=pl.ANY)
F32 = jnp.float32
BF16 = jnp.bfloat16
MIB = 2**20
FIRST_SPLIT = (3,)
SECOND_SPLIT = (3,)
PIECES = 1


def shape(dims, dtype):
    return jax.ShapeDtypeStruct(dims, dtype)


def call(kernel, outs, in_specs, scratch=(), limit=6, flops=0, moved=0, loads=(), ordered=()):
    n_in, n_out, n_load, n_held = len(in_specs), len(outs), len(loads), len(loads) + len(ordered)

    def body(*refs):
        ins, sources, outs = refs[:n_in], refs[n_in : n_in + n_load], refs[n_in + n_held :]
        targets, rest = outs[n_out : n_out + n_load], outs[n_out + n_load :]
        copies = [
            pltpu.make_async_copy(source.at[window], target, rest[-1].at[i])
            for i, (source, target, (_, window, _)) in enumerate(zip(sources, targets, loads))
        ]
        for copy in copies:
            copy.start()
        kernel(*ins, *outs[:n_out], *rest[: len(scratch)])
        for copy in copies:
            copy.wait()

    function = pl.pallas_call(
        body,
        out_shape=list(outs) + [pltpu.VMEM(dims, a.dtype) for a, _, dims in loads],
        in_specs=list(in_specs) + [ANY] * n_held,
        out_specs=[VMEM] * n_out + [ANY] * n_load,
        scratch_shapes=list(scratch) + ([pltpu.SemaphoreType.DMA((n_load,))] if loads else []),
        compiler_params=pltpu.CompilerParams(vmem_limit_bytes=limit * MIB),
        cost_estimate=pl.CostEstimate(
            flops=flops,
            bytes_accessed=moved + sum(2 * math.prod(dims) for _, _, dims in loads),
            transcendentals=0,
        ),
    )
    held = [pltpu.with_memory_space_constraint(a, pltpu.HBM) for a, _, _ in loads]
    return lambda *operands: function(*operands, *held, *ordered)


def whole(array):
    return array, tuple(slice(None) for _ in array.shape), array.shape


def load_kernel(after_ref):
    pass


def load(loads, after):
    moved = sum(math.prod(dims) for _, _, dims in loads)
    return call(load_kernel, [], [ANY], limit=2, flops=moved * 200, loads=loads)(after)


def chunks(width):
    size = min(512, width)
    return [slice(c, c + size) for c in range(0, width, size)]


def tail_of(squares):
    lane = lax.broadcasted_iota(jnp.int32, (squares.shape[0], LANES), 1)
    high = squares.astype(BF16).astype(F32)
    middle = (squares - high).astype(BF16).astype(F32)
    low = squares - high - middle
    return jnp.where(lane == 0, high, jnp.where(lane == 1, middle, jnp.where(lane == 2, low, 0.0)))


def deliver(value, at, own_ref, sends):
    block = own_ref.shape[0]
    own_ref[:, at] = value[:block]
    for e, send in enumerate(sends, 1):
        send[:, at] = value[e * block : (e + 1) * block].astype(BF16)


def slot_onehot(placement, slots):
    batch = placement.shape[1]
    at = lax.broadcasted_iota(jnp.int32, (batch, batch), 0)
    slot = (lax.axis_index(GROUP) ^ (at // slots)) * slots + at % slots
    return (slot == placement).astype(F32).astype(BF16)


def head_kernel(out_ref):
    out_ref[...] = jnp.zeros_like(out_ref)


def first_kernel(n_t, products, *refs):
    parts, (placement_ref, gain_ref, w_ref) = refs[:n_t], refs[n_t : n_t + 3]
    x_ref, gained_ref, own_ref, *sends = refs[n_t + 3 :]
    rows = parts[0].shape[0]
    t = lax.axis_index("tensor")
    for d in range(n_t):
        at = pl.multiple_of((t ^ d) * rows, rows)
        x_ref[pl.ds(at, rows), :] = parts[d][...].astype(F32)
    onehot = slot_onehot(placement_ref[...], own_ref.shape[0])
    xp = jnp.dot(onehot, x_ref[...].astype(BF16), preferred_element_type=F32)
    gained = (xp * gain_ref[...]).astype(BF16)
    gained_ref[...] = gained
    tail = tail_of(jnp.sum(xp * xp, axis=1, keepdims=True))
    width = w_ref.shape[2]
    deliver(tail, slice(products * width, products * width + LANES), own_ref, sends)
    for j in range(products):
        for c in chunks(width):
            out = jnp.dot(gained, w_ref[j, :, c], preferred_element_type=F32)
            deliver(out, slice(j * width + c.start, j * width + c.stop), own_ref, sends)


def more_kernel(start, products, gained_ref, w_ref, own_ref, *sends):
    width = w_ref.shape[2]
    gained = gained_ref[...]
    for j in range(products):
        for c in chunks(width):
            out = jnp.dot(gained, w_ref[start + j, :, c], preferred_element_type=F32)
            deliver(out, slice(j * width + c.start, j * width + c.stop), own_ref, sends)


def collect(features, width, n_g, counts, refs):
    products = []
    for i, count in enumerate(counts):
        own_ref, *received = refs[i * n_g : (i + 1) * n_g]
        total = own_ref[...]
        for ref in received:
            total = total + ref[...].astype(F32)
        products += [total[:, j * width : (j + 1) * width] for j in range(count)]
        if i == 0:
            squares = jnp.sum(total[:, count * width :], axis=1, keepdims=True)
            scale = lax.rsqrt(squares / features + EPS)
    return [p * scale for p in products]


def attend_kernel(n_g, features, counts, *refs):
    n = n_g * len(counts)
    lengths_ref, keys_ref, values_ref, out_ref = refs[n:]
    slots, width = out_ref.shape
    columns = keys_ref.shape[0]
    positions = columns // slots
    query, fresh_key, fresh_value = [
        p.astype(BF16).astype(F32) for p in collect(features, width, n_g, counts, refs[:n])
    ]
    scale = 1.0 / math.sqrt(HEAD_DIM)
    column = lax.broadcasted_iota(jnp.int32, (slots, columns), 1)
    slot = lax.broadcasted_iota(jnp.int32, (slots, columns), 0)
    length = jnp.zeros((slots, columns), jnp.int32)
    for s in range(slots):
        length = jnp.where(slot == s, lengths_ref[s], length)
    live = (column >= slot * positions) & (column < slot * positions + length)
    heads = [slice(h, h + HEAD_DIM) for h in range(0, width, HEAD_DIM)]
    scores = [
        scale
        * lax.dot_general(
            query[:, h].astype(BF16), keys_ref[:, h], (((1,), (1,)), ((), ())), preferred_element_type=F32
        )
        for h in heads
    ]
    own_scores = [scale * jnp.sum(query[:, h] * fresh_key[:, h], axis=1, keepdims=True) for h in heads]
    mixed = []
    for h, score, own_score in zip(heads, scores, own_scores):
        top = jnp.maximum(jnp.max(jnp.where(live, score, -jnp.inf), axis=1, keepdims=True), own_score)
        probs = jnp.where(live, jnp.exp(score - top), 0.0)
        self_prob = jnp.exp(own_score - top)
        total = jnp.sum(probs, axis=1, keepdims=True) + self_prob
        weights = (probs / total).astype(BF16)
        self_weight = (self_prob / total).astype(BF16).astype(F32)
        out = jnp.dot(weights, values_ref[:, h], preferred_element_type=F32)
        out_ref[:, h] = (out + self_weight * fresh_value[:, h]).astype(BF16)


def out_kernel(n_g, pieces, *refs):
    parts, (placement_ref, w_ref) = refs[:n_g], refs[n_g : n_g + 2]
    owns, sends = refs[n_g + 2 :: 2], refs[n_g + 3 :: 2]
    gathered = jnp.concatenate([p[...].astype(F32) for p in parts], axis=0).astype(BF16)
    onehot = slot_onehot(placement_ref[...], parts[0].shape[0])
    rows = lax.dot_general(
        onehot, gathered, (((0,), (0,)), ((), ())), preferred_element_type=F32
    ).astype(BF16)
    width = w_ref.shape[1] // pieces
    for own_ref, send_ref, start in zip(owns, sends, range(0, w_ref.shape[1], width)):
        for c in chunks(width):
            out = jnp.dot(
                rows, w_ref[:, start + c.start : start + c.stop], preferred_element_type=F32
            )
            own_ref[:, c] = out
            send_ref[:, c] = out.astype(BF16)


def join(n_t, n_g, block, piece, x_ref, terms_ref, received, gain_ref, attended_ref, scratch):
    rows, width = attended_ref.shape
    columns = slice(piece * width, (piece + 1) * width)
    total = terms_ref[...]
    for ref in received:
        total = total + ref[...].astype(F32)
    scratch[...] = (x_ref[:, columns] + total).astype(BF16).astype(F32)
    at = pl.multiple_of(lax.axis_index("tensor") * rows, rows)
    attended_ref[...] = scratch[pl.ds(at, rows), :].astype(BF16)
    g = lax.axis_index(GROUP)
    xp = jnp.concatenate(
        [scratch[pl.ds(pl.multiple_of((g ^ e) * block, block), block), :] for e in range(n_g)], axis=0
    )
    return jnp.sum(xp * xp, axis=1, keepdims=True), (xp * gain_ref[:, columns]).astype(BF16)


def piece_kernel(n_t, n_g, block, piece, *refs):
    x_ref, terms_ref, *received = refs[: n_t + 1]
    gain_ref, w_ref = refs[n_t + 1 : n_t + 3]
    before, (attended_ref, sums_ref, squares_ref, scratch) = refs[n_t + 3 : -4], refs[-4:]
    squares, gained = join(
        n_t, n_g, block, piece, x_ref, terms_ref, received, gain_ref, attended_ref, scratch
    )
    squares_ref[...] = (before[1][...] if before else 0.0) + jnp.broadcast_to(squares, squares_ref.shape)
    width = w_ref.shape[2]
    for j in range(3):
        for c in chunks(width):
            at = slice(j * width + c.start, j * width + c.stop)
            out = jnp.dot(gained, w_ref[j, :, c], preferred_element_type=F32)
            sums_ref[:, at] = out + before[0][:, at] if before else out


def last_kernel(n_t, n_g, piece, products, *refs):
    x_ref, terms_ref, *received = refs[: n_t + 1]
    gain_ref, w_ref = refs[n_t + 1 : n_t + 3]
    before = refs[n_t + 3 : -(n_g + 3)]
    attended_ref, gained_ref, own_ref, *sends, scratch = refs[-(n_g + 3) :]
    squares, gained = join(
        n_t, n_g, own_ref.shape[0], piece, x_ref, terms_ref, received, gain_ref, attended_ref, scratch
    )
    gained_ref[...] = gained
    if before:
        squares = squares + before[1][:, :1]
    width = w_ref.shape[2]
    deliver(
        tail_of(squares), slice(products * width, products * width + LANES), own_ref, sends
    )
    for j in range(products):
        for c in chunks(width):
            at = slice(j * width + c.start, j * width + c.stop)
            out = jnp.dot(gained, w_ref[j, :, c], preferred_element_type=F32)
            deliver(out + before[0][:, at] if before else out, at, own_ref, sends)


def tail_products_kernel(n_g, start, products, *refs):
    gained_ref, w_ref, *before = refs[:-n_g]
    own_ref, *sends = refs[-n_g:]
    width = w_ref.shape[2]
    gained = gained_ref[...]
    for j in range(products):
        for c in chunks(width):
            out = jnp.dot(gained, w_ref[start + j, :, c], preferred_element_type=F32)
            if before:
                at = (start + j) * width
                out = out + before[0][:, at + c.start : at + c.stop]
            deliver(out, slice(j * width + c.start, j * width + c.stop), own_ref, sends)


def mixer_kernel(n_g, features, counts, *refs):
    n = n_g * len(counts)
    outer_taps, outer_state, inner_taps, inner_state, out_ref = refs[n:]
    branches = collect(features, out_ref.shape[1], n_g, counts, refs[:n])
    conv = [
        outer_taps[0, j : j + 1] * branches[j]
        + outer_taps[1, j : j + 1] * outer_state[0, j].astype(F32)
        + outer_taps[2, j : j + 1] * outer_state[1, j].astype(F32)
        for j in range(3)
    ]
    filtered = (
        inner_taps[0:1] * (conv[0] * conv[2])
        + inner_taps[1:2] * inner_state[0].astype(F32)
        + inner_taps[2:3] * inner_state[1].astype(F32)
    )
    out_ref[...] = (conv[1] * filtered).astype(BF16)


def local(
    n_t,
    n_g,
    residual,
    attn_gain,
    attn_proj,
    cache_keys,
    cache_values,
    lengths,
    placement,
    out_proj,
    mix_gain,
    mix_proj,
    outer_taps,
    outer_state,
    inner_taps,
    inner_state,
):
    rows, depth = residual.shape
    slots = lengths.shape[0]
    batch = placement.shape[0]
    width = attn_proj.shape[2]
    features = depth * n_g
    placement = placement.reshape(1, batch)
    attn_gain, mix_gain = attn_gain.reshape(1, depth), mix_gain.reshape(1, depth)

    def swap(x, axes, n):
        return [lax.ppermute(x[d - 1], axes, [(i, i ^ d) for i in range(n)]) for d in range(1, n)]

    def blocks(products, tail):
        columns = products * width + tail
        return [shape((slots, columns), F32)] + [shape((slots, columns), BF16)] * (n_g - 1)

    def cost(k, n):
        return dict(flops=2 * batch * k * n, moved=2 * k * n)

    (head,) = call(head_kernel, [shape((8, LANES), F32)], [], limit=2, flops=attn_proj.size * 64 * 40, moved=attn_proj.size * 80)()
    residual, head = lax.optimization_barrier((residual, head))
    parts = [residual] + swap([residual] * n_t, "tensor", n_t)
    attn_w = pltpu.with_memory_space_constraint(attn_proj, pltpu.VMEM)
    count = FIRST_SPLIT[0]
    keys, values = [c.reshape(-1, width) for c in (cache_keys, cache_values)]
    x, gained, own, *sends, keys, values, out_w = call(
        functools.partial(first_kernel, n_t, count),
        [shape((batch, depth), F32), shape((batch, depth), BF16)] + blocks(count, LANES),
        [VMEM] * (n_t + 3),
        **cost(depth, count * width),
        loads=[whole(keys), whole(values), whole(out_proj)],
        ordered=[head],
    )(*parts, placement, attn_gain, attn_w)
    arrived = [own] + swap(sends, GROUP, n_g)
    start = count
    for count in FIRST_SPLIT[1:]:
        own, *sends = call(
            functools.partial(more_kernel, start, count),
            blocks(count, 0),
            [VMEM] * 2,
            **cost(depth, count * width),
        )(gained, attn_w)
        arrived += [own] + swap(sends, GROUP, n_g)
        start += count

    part = depth // PIECES
    def piece_of(p):
        return mix_proj, (slice(None), slice(p * part, (p + 1) * part), slice(None)), (3, part, width)

    (slot_out,) = call(
        functools.partial(attend_kernel, n_g, features, FIRST_SPLIT),
        [shape((slots, width), BF16)],
        [VMEM] * len(arrived) + [SMEM, VMEM, VMEM],
        flops=4 * cache_keys.size,
        moved=cache_keys.size * 4,
        ordered=(),
    )(*arrived, lengths, keys, values)

    gathered = [slot_out] + swap([slot_out] * n_g, GROUP, n_g)
    terms = call(
        functools.partial(out_kernel, n_g, PIECES),
        [shape((batch, part), F32), shape((batch, part), BF16)] * PIECES,
        [VMEM] * (n_g + 2),
        **cost(width, depth),
        ordered=(),
    )(*gathered, placement, out_w)

    received = [swap([terms[2 * p + 1]] * n_t, "tensor", n_t) for p in range(PIECES)]
    mix_w = load([piece_of(p) for p in range(PIECES)], terms[0])
    attended, before = [], []
    for p in range(PIECES - 1):
        out, *before = call(
            functools.partial(piece_kernel, n_t, n_g, slots, p),
            [shape((rows, part), BF16), shape((batch, 3 * width), F32), shape((batch, LANES), F32)],
            [VMEM] * (n_t + 3 + len(before)),
            scratch=[pltpu.VMEM((batch, part), F32)],
            **cost(part, 3 * width),
        )(x, terms[2 * p], *received[p], mix_gain, mix_w[p], *before)
        attended.append(out)
    count = SECOND_SPLIT[0]
    out, gained, own, *sends = call(
        functools.partial(last_kernel, n_t, n_g, PIECES - 1, count),
        [shape((rows, part), BF16), shape((batch, part), BF16)] + blocks(count, LANES),
        [VMEM] * (n_t + 3 + len(before)),
        scratch=[pltpu.VMEM((batch, part), F32)],
        **cost(part, count * width),
    )(x, terms[-2], *received[-1], mix_gain, mix_w[-1], *before)
    attended.append(out)
    arrived = [own] + swap(sends, GROUP, n_g)
    start = count
    for count in SECOND_SPLIT[1:]:
        own, *sends = call(
            functools.partial(tail_products_kernel, n_g, start, count),
            blocks(count, 0),
            [VMEM] * (2 + len(before[:1])),
            **cost(part, count * width),
        )(gained, mix_w[-1], *before[:1])
        arrived += [own] + swap(sends, GROUP, n_g)
        start += count
    (gated,) = call(
        functools.partial(mixer_kernel, n_g, features, SECOND_SPLIT),
        [shape((slots, width), BF16)],
        [VMEM] * (len(arrived) + 4),
        flops=slots * width * 40,
        moved=slots * width * 40,
    )(*arrived, outer_taps, outer_state, inner_taps, inner_state)
    return (jnp.concatenate(attended, axis=1), gated)


def solution(mesh):
    n_t = mesh.shape["tensor"]
    n_g = mesh.shape["rows"] * mesh.shape["role"]
    for n in (n_t, n_g):
        assert n & (n - 1) == 0, "axis size"
    return jax.shard_map(
        functools.partial(local, n_t, n_g),
        mesh=mesh,
        in_specs=(
            P(("groups", "tensor"), ("rows", "role")),
            P(("rows", "role")),
            P(None, ("rows", "role"), "tensor"),
            P(("groups", "rows", "role"), None, "tensor"),
            P(("groups", "rows", "role"), None, "tensor"),
            P(("groups", "rows", "role")),
            P("groups"),
            P("tensor", ("rows", "role")),
            P(("rows", "role")),
            P(None, ("rows", "role"), "tensor"),
            P(None, None, "tensor"),
            P(None, None, ("groups", "rows", "role"), "tensor"),
            P(None, "tensor"),
            P(None, ("groups", "rows", "role"), "tensor"),
        ),
        out_specs=(
            P(("groups", "tensor"), ("rows", "role")),
            P(("groups", "rows", "role"), "tensor"),
        ),
        check_vma=False,
    )
```

time: 158 us -> 58.1 us (0.37)
  blocking collectives: 65.4 us -> 0 us
  matrix products: 27 us -> 0 us
  Pallas kernels: 0 us -> 22.2 us
  waiting for transfers between devices: 39.3 us -> 18.3 us
  starting transfers between devices: 0.08 us -> 15.9 us
  between operations: 14.3 us -> 0.78 us
  other arithmetic: 6.88 us -> 0 us
  local copies, waits for them, and re-layouts: 4.83 us -> 0.76 us
    psum x3 -> x0, blocking collectives: 32.9 us -> none  [the longest x1 18.9 us: local(): full = lax.psum(terms, ('rows', 'role'))]
    all_gather x3 -> x0, blocking collectives: 32.5 us -> none  [the longest x1 13.6 us: local(): lax.all_gather(normed, 'tensor', axis=0, tiled=True)]
    dot_general x5 -> x0, matrix products: 27 us -> none  [the longest x1 10.5 us: local(): jnp.einsum('rd,jde->jre', lax.all_gather(mix_normed, 'tensor', axis=0, ti...]
    pallas_call x0 -> x7, Pallas kernels: none -> 22.2 us  [call(): return lambda *operands: function(*operands, *held, *ordered)]
    reduce_scatter x1 -> x0, waiting for transfers between devices: 19.9 us -> none  [local(): lax.psum_scatter(token_terms.astype(jnp.bfloat16), 'tensor', scatter_dime...]
    unnamed x3 -> x0, waiting for transfers between devices: 19.4 us -> none
    ppermute x0 -> x15, waiting for transfers between devices: none -> 18.3 us  [swap(): lax.ppermute(x[d - 1], axes, [(i, i ^ d) for i in range(n)])]
    ppermute x0 -> x15, starting transfers between devices: none -> 15.9 us  [swap(): lax.ppermute(x[d - 1], axes, [(i, i ^ d) for i in range(n)])]
  transfers between devices with their start and end apart: 2 -> 15, of which waited for: 2 -> 9; matrix products, arithmetic and copies ran while one was open for 0% -> 0% of each run, Pallas kernels for 0% -> 14%
where the time goes in v2:
time: 58.1 us; the launch traced here: 57.9 us
  Pallas kernels  22.2 us (38%)
  waiting for transfers between devices  18.3 us (31%)
  starting transfers between devices  15.9 us (27%)
  between operations  0.78 us (1%)
  local copies, waits for them, and re-layouts  0.76 us (1%)
    pallas_call x7, Pallas kernels, call(): return lambda *operands: function(*operands, *held, *ordered)  22.2 us
    ppermute x15, waiting for transfers between devices, swap(): lax.ppermute(x[d - 1], axes, [(i, i ^ d) for i in range(n)])  18.3 us
    ppermute x15, starting transfers between devices, swap(): lax.ppermute(x[d - 1], axes, [(i, i ^ d) for i in range(n)])  15.9 us
  transfers between devices with their start and end apart: 15, of which 9 were waited for; matrix products, arithmetic and copies ran while one was open for 0% of the time, Pallas kernels for 14%

profile of v2, /device:TPU:0, one launch (start us, length us, event | category | flops | bytes accessed | tf_op | source)
XLA Modules:
  0.0 57.9 jit_solution(1097481519749378848)
XLA Ops:
  0.6 0.0 copy-start.5
  0.6 0.0 copy-start.8
  0.7 0.0 copy-start
  0.7 0.0 copy-start.7
  0.7 0.7 %copy-done.5 = bf16[8,2048]{1,0:T(8,128)(2,1)S(1)} copy-done((bf16[8,2048]{1,0:T(8,128)(2,1)S(1)}, bf16[8,2048]{1,0:T(8,128)(2,1)}, u32[]{:S(2)}) %copy-start.5) | copy-done | bytes 32792
  1.4 5.1 %collective-permute-start.2 = (bf16[8,2048]{1,0:T(8,128)(2,1)S(1)}, bf16[8,2048]{1,0:T(8,128)(2,1)S(1)}, u32[]{:S(2)}, u32[]{:S(2)}) collective-permute-start(bf16[8,2048]{1,0:T(8,128)(2,1)S(1)} %copy-done.5), channel_id=1, source_target_pairs={{0,12},{4,8},{8,4},{12,0},{1,13},{5,9},{9,5},{13,1},{2,14},{6,10},... | collective-permute-start | bytes 98312 | tf_op jit(solution)/shard_map/ppermute | solution.py:319
  6.5 0.0 collective-permute-start.1
  6.5 0.6 collective-permute-start
  7.0 1.3 %collective-permute-done.2.refs_3_ = bf16[8,2048]{1,0:T(8,128)(2,1)S(1)} collective-permute-done((bf16[8,2048]{1,0:T(8,128)(2,1)S(1)}, bf16[8,2048]{1,0:T(8,128)(2,1)S(1)}, u32[]{:S(2)}, u32[]{:S(2)}) %collective-permute-start.2) | collective-permute-done | bytes 32800 | tf_op jit(solution)/shard_map/ppermute | solution.py:319
  8.4 2.9 %collective-permute-done.1.refs_2_ = bf16[8,2048]{1,0:T(8,128)(2,1)S(1)} collective-permute-done((bf16[8,2048]{1,0:T(8,128)(2,1)S(1)}, bf16[8,2048]{1,0:T(8,128)(2,1)S(1)}, u32[]{:S(2)}, u32[]{:S(2)}) %collective-permute-start.1) | collective-permute-done | bytes 32800 | tf_op jit(solution)/shard_map/ppermute | solution.py:319
  11.3 0.0 collective-permute-done.refs_1_
  11.3 0.0 copy-done.8
  11.3 5.3 %shard_map.150 = (f32[32,2048]{1,0:T(8,128)S(1)}, bf16[32,2048]{1,0:T(8,128)(2,1)}, f32[8,6272]{1,0:T(8,128)S(1)}, bf16[8,6272]{1,0:T(8,128)(2,1)S(1)}, bf16[8,6...) custom-call(bf16[8,2048]{1,0:T(8,128)(2,1)S(1)} %copy-done.5, ...), custom_call_target="tpu_custom_call" | custom-call | flops 805306368 | bytes 35651584 | tf_op jit(solution)/shard_map/pallas_call | solution.py:60
  16.6 0.1 collective-permute-start.3
  16.7 1.6 %collective-permute-start.4 = (bf16[8,6272]{1,0:T(8,128)(2,1)S(1)}, bf16[8,6272]{1,0:T(8,128)(2,1)S(1)}, u32[]{:S(2)}, u32[]{:S(2)}) collective-permute-start(bf16[8,6272]{1,0:T(8,128)(2,1)S(1)} %get-tuple-element.24), channel_id=1, source_target_pairs={{0,2},{1,3},{2,0},{3,1},{4,6},{5,7},{6,4},{7,5},{8,10},{9,11},{10,... | collective-permute-start | bytes 301064 | tf_op jit(solution)/shard_map/ppermute | solution.py:319
  18.2 0.3 collective-permute-start.5
  18.5 0.0 collective-permute-done.3.refs_1_
  18.5 3.9 %collective-permute-done.4.refs_2_ = bf16[8,6272]{1,0:T(8,128)(2,1)S(1)} collective-permute-done((bf16[8,6272]{1,0:T(8,128)(2,1)S(1)}, bf16[8,6272]{1,0:T(8,128)(2,1)S(1)}, u32[]{:S(2)}, u32[]{:S(2)}) %collective-permute-start.4) | collective-permute-done | bytes 100384 | tf_op jit(solution)/shard_map/ppermute | solution.py:319
  22.5 1.1 %collective-permute-done.5.refs_3_ = bf16[8,6272]{1,0:T(8,128)(2,1)S(1)} collective-permute-done((bf16[8,6272]{1,0:T(8,128)(2,1)S(1)}, bf16[8,6272]{1,0:T(8,128)(2,1)S(1)}, u32[]{:S(2)}, u32[]{:S(2)}) %collective-permute-start.5) | collective-permute-done | bytes 100384 | tf_op jit(solution)/shard_map/ppermute | solution.py:319
  23.5 0.0 copy-done.9
  23.5 1.3 %shard_map.151.refs_0_ = bf16[8,2048]{1,0:T(8,128)(2,1)S(1)} custom-call(f32[8,6272]{1,0:T(8,128)S(1)} %get-tuple-element.22.refs_0_, bf16[8,6272]{1,0:T(8,128)(2,1)S(1)} %collective-permute-done.3.refs_1_, bf16[8,6272]{1,0:T(8,128)(2,1)S(1)} %collective-permute-done.4.refs_2_, bf16[8,6272]{1,0:T(8,128)(2,1)S(1)} %collective-permute-done.5.refs_3_, ...), custom_call_target="tpu_custom_call" | custom-call | flops 2097152 | bytes 2097152 | tf_op jit(solution)/shard_map/pallas_call | solution.py:60
  24.8 1.5 %collective-permute-start.8 = (bf16[8,2048]{1,0:T(8,128)(2,1)S(1)}, bf16[8,2048]{1,0:T(8,128)(2,1)S(1)}, u32[]{:S(2)}, u32[]{:S(2)}) collective-permute-start(bf16[8,2048]{1,0:T(8,128)(2,1)S(1)} %shard_map.151.refs_0_), channel_id=1, source_target_pairs={{0,3},{1,2},{2,1},{3,0},{4,7},{5,6},{6,5},{7,4},{8,11},{9,10},{10,... | collective-permute-start | bytes 98312 | tf_op jit(solution)/shard_map/ppermute | solution.py:319
  26.3 0.5 collective-permute-start.7
  26.8 0.0 collective-permute-start.6
  26.8 1.3 %collective-permute-done.8.refs_3_ = bf16[8,2048]{1,0:T(8,128)(2,1)S(1)} collective-permute-done((bf16[8,2048]{1,0:T(8,128)(2,1)S(1)}, bf16[8,2048]{1,0:T(8,128)(2,1)S(1)}, u32[]{:S(2)}, u32[]{:S(2)}) %collective-permute-start.8) | collective-permute-done | bytes 32800 | tf_op jit(solution)/shard_map/ppermute | solution.py:319
  28.2 2.0 %collective-permute-done.7.refs_2_ = bf16[8,2048]{1,0:T(8,128)(2,1)S(1)} collective-permute-done((bf16[8,2048]{1,0:T(8,128)(2,1)S(1)}, bf16[8,2048]{1,0:T(8,128)(2,1)S(1)}, u32[]{:S(2)}, u32[]{:S(2)}) %collective-permute-start.7) | collective-permute-done | bytes 32800 | tf_op jit(solution)/shard_map/ppermute | solution.py:319
  30.2 0.0 collective-permute-done.6.refs_1_
  30.2 1.7 %shard_map.152 = (f32[32,2048]{1,0:T(8,128)S(1)}, bf16[32,2048]{1,0:T(8,128)(2,1)S(1)}) custom-call(bf16[8,2048]{1,0:T(8,128)(2,1)S(1)} %shard_map.151.refs_0_, bf16[8,2048]{1,0:T(8,128)(2,1)S(1)} %collective-permute-done.6.refs_1_, bf16[8,2048]{1,0:T(8,128)(2,1)S(1)} %collective-permute-done.7.refs_2_, bf16[8,2048]{1,0:T(8,128)(2,1)S(1)} %collective-permute-done.8.refs_3_, ...), custom_call_target="tpu_custom_call" | custom-call | flops 268435456 | bytes 8388608 | tf_op jit(solution)/shard_map/pallas_call | solution.py:60
  31.9 2.6 %collective-permute-start.11 = (bf16[32,2048]{1,0:T(8,128)(2,1)S(1)}, bf16[32,2048]{1,0:T(8,128)(2,1)S(1)}, u32[]{:S(2)}, u32[]{:S(2)}) collective-permute-start(bf16[32,2048]{1,0:T(8,128)(2,1)S(1)} %get-tuple-element.30), channel_id=1, source_target_pairs={{0,12},{4,8},{8,4},{12,0},{1,13},{5,9},{9,5},{13,1},{2,14},{6,10},... | collective-permute-start | bytes 393224 | tf_op jit(solution)/shard_map/ppermute | solution.py:319
  34.5 0.0 collective-permute-start.10
  34.5 1.8 %collective-permute-start.9 = (bf16[32,2048]{1,0:T(8,128)(2,1)S(1)}, bf16[32,2048]{1,0:T(8,128)(2,1)S(1)}, u32[]{:S(2)}, u32[]{:S(2)}) collective-permute-start(bf16[32,2048]{1,0:T(8,128)(2,1)S(1)} %get-tuple-element.30), channel_id=1, source_target_pairs={{0,4},{4,0},{8,12},{12,8},{1,5},{5,1},{9,13},{13,9},{2,6},{6,2},{1... | collective-permute-start | bytes 393224 | tf_op jit(solution)/shard_map/ppermute | solution.py:319
  36.3 8.2 %shard_map.153.refs_6_ = bf16[3,2048,2048]{2,1,0:T(8,128)(2,1)S(1)} custom-call(f32[32,2048]{1,0:T(8,128)S(1)} %get-tuple-element.29.refs_0_.refs_1_, bf16[3,2048,2048]{2,1,0:T(8,128)(2,1)} %refs_1_.1), custom_call_target="tpu_custom_call" | custom-call | flops 2516582400 | bytes 25165824 | tf_op jit(solution)/shard_map/pallas_call | solution.py:60
  44.5 0.0 copy-start.1
  44.5 0.0 copy-start.2
  44.5 0.0 copy-start.3
  44.6 0.0 copy-start.4
  44.6 0.0 collective-permute-done.11.refs_4_
  44.6 0.6 %collective-permute-done.10.refs_3_ = bf16[32,2048]{1,0:T(8,128)(2,1)S(1)} collective-permute-done((bf16[32,2048]{1,0:T(8,128)(2,1)S(1)}, bf16[32,2048]{1,0:T(8,128)(2,1)S(1)}, u32[]{:S(2)}, u32[]{:S(2)}) %collective-permute-start.10) | collective-permute-done | bytes 131104 | tf_op jit(solution)/shard_map/ppermute | solution.py:319
  45.2 0.0 collective-permute-done.9.refs_2_
  45.2 5.0 %shard_map.154 = (bf16[8,2048]{1,0:T(8,128)(2,1)}, bf16[32,2048]{1,0:T(8,128)(2,1)}, f32[8,6272]{1,0:T(8,128)S(1)}, bf16[8,6272]{1,0:T(8,128)(2,1)S(1)}, bf16[8,...) custom-call(f32[32,2048]{1,0:T(8,128)S(1)} %get-tuple-element.21.refs_0_, ...), custom_call_target="tpu_custom_call" | custom-call | flops 805306368 | bytes 25165824 | tf_op jit(solution)/shard_map/pallas_call | solution.py:60
  50.2 0.0 collective-permute-start.12
  50.2 0.9 %collective-permute-start.13 = (bf16[8,6272]{1,0:T(8,128)(2,1)S(1)}, bf16[8,6272]{1,0:T(8,128)(2,1)S(1)}, u32[]{:S(2)}, u32[]{:S(2)}) collective-permute-start(bf16[8,6272]{1,0:T(8,128)(2,1)S(1)} %get-tuple-element.34), channel_id=1, source_target_pairs={{0,2},{1,3},{2,0},{3,1},{4,6},{5,7},{6,4},{7,5},{8,10},{9,11},{10,... | collective-permute-start | bytes 301064 | tf_op jit(solution)/shard_map/ppermute | solution.py:319
  51.1 1.0 %collective-permute-start.14 = (bf16[8,6272]{1,0:T(8,128)(2,1)S(1)}, bf16[8,6272]{1,0:T(8,128)(2,1)S(1)}, u32[]{:S(2)}, u32[]{:S(2)}) collective-permute-start(bf16[8,6272]{1,0:T(8,128)(2,1)S(1)} %get-tuple-element.35), channel_id=1, source_target_pairs={{0,3},{1,2},{2,1},{3,0},{4,7},{5,6},{6,5},{7,4},{8,11},{9,10},{10,... | collective-permute-start | bytes 301064 | tf_op jit(solution)/shard_map/ppermute | solution.py:319
  52.1 0.0 collective-permute-done.12.refs_1_
  52.1 3.9 %collective-permute-done.13.refs_2_ = bf16[8,6272]{1,0:T(8,128)(2,1)S(1)} collective-permute-done((bf16[8,6272]{1,0:T(8,128)(2,1)S(1)}, bf16[8,6272]{1,0:T(8,128)(2,1)S(1)}, u32[]{:S(2)}, u32[]{:S(2)}) %collective-permute-start.13) | collective-permute-done | bytes 100384 | tf_op jit(solution)/shard_map/ppermute | solution.py:319
  55.9 1.2 %collective-permute-done.14.refs_3_ = bf16[8,6272]{1,0:T(8,128)(2,1)S(1)} collective-permute-done((bf16[8,6272]{1,0:T(8,128)(2,1)S(1)}, bf16[8,6272]{1,0:T(8,128)(2,1)S(1)}, u32[]{:S(2)}, u32[]{:S(2)}) %collective-permute-start.14) | collective-permute-done | bytes 100384 | tf_op jit(solution)/shard_map/ppermute | solution.py:319
  57.2 0.0 copy-done.2
  57.2 0.8 %shard_map.155 = bf16[8,2048]{1,0:T(8,128)(2,1)} custom-call(f32[8,6272]{1,0:T(8,128)S(1)} %get-tuple-element.32.refs_0_, bf16[8,6272]{1,0:T(8,128)(2,1)S(1)} %collective-permute-done.12.refs_1_, bf16[8,6272]{1,0:T(8,128)(2,1)S(1)} %collective-permute-done.13.refs_2_, bf16[8,6272]{1,0:T(8,128)(2,1)S(1)} %collective-permute-done.14.refs_3_, ...), custom_call_target="tpu_custom_call" | custom-call | flops 655360 | bytes 655360 | tf_op jit(solution)/shard_map/pallas_call | solution.py:60
  (9 shorter events, 0.0 us)
Async XLA Ops:
  0.6 0.8 %copy-start.5 = (bf16[8,2048]{1,0:T(8,128)(2,1)S(1)}, bf16[8,2048]{1,0:T(8,128)(2,1)}, u32[]{:S(2)}) copy-start(bf16[8,2048]{1,0:T(8,128)(2,1)} %refs_0_) | copy-start | bytes 98308
  0.6 10.6 %copy-start.8 = (s32[32]{0:T(128)S(1)}, s32[32]{0:T(128)}, u32[]{:S(2)}) copy-start(s32[32]{0:T(128)} %param.20) | copy-start | bytes 388
  0.7 10.6 %copy-start = (bf16[3,2048,2048]{2,1,0:T(8,128)(2,1)S(1)}, bf16[3,2048,2048]{2,1,0:T(8,128)(2,1)}, u32[]{:S(2)}) copy-start(bf16[3,2048,2048]{2,1,0:T(8,128)(2,1)} %refs_6_.2) | copy-start | bytes 75497472
  0.7 10.6 %copy-start.7 = (f32[2048]{0:T(1024)S(1)}, f32[2048]{0:T(1024)}, u32[]{:S(2)}) copy-start(f32[2048]{0:T(1024)} %param.15) | copy-start | bytes 24580
  1.4 22.1 %copy-start.9 = (s32[8]{0:T(128)S(1)}, s32[8]{0:T(128)}, u32[]{:S(2)}) copy-start(s32[8]{0:T(128)} %refs_4_.2) | copy-start | bytes 100
  1.4 7.0 %collective-permute-start.2 = (bf16[8,2048]{1,0:T(8,128)(2,1)S(1)}, bf16[8,2048]{1,0:T(8,128)(2,1)S(1)}, u32[]{:S(2)}, u32[]{:S(2)}) collective-permute-start(bf16[8,2048]{1,0:T(8,128)(2,1)S(1)} %copy-done.5), channel_id=1, source_target_pairs={{0,12},{4,8},{8,4},{12,0},{1,13},{5,9},{9,5},{13,1},{2,14},{6,10},... | collective-permute-start | bytes 98312 | tf_op jit(solution)/shard_map/ppermute | solution.py:319
  6.5 4.8 %collective-permute-start.1 = (bf16[8,2048]{1,0:T(8,128)(2,1)S(1)}, bf16[8,2048]{1,0:T(8,128)(2,1)S(1)}, u32[]{:S(2)}, u32[]{:S(2)}) collective-permute-start(bf16[8,2048]{1,0:T(8,128)(2,1)S(1)} %copy-done.5), channel_id=1, source_target_pairs={{0,8},{4,12},{8,0},{12,4},{1,9},{5,13},{9,1},{13,5},{2,10},{6,14},... | collective-permute-start | bytes 98312 | tf_op jit(solution)/shard_map/ppermute | solution.py:319
  6.5 4.8 %collective-permute-start = (bf16[8,2048]{1,0:T(8,128)(2,1)S(1)}, bf16[8,2048]{1,0:T(8,128)(2,1)S(1)}, u32[]{:S(2)}, u32[]{:S(2)}) collective-permute-start(bf16[8,2048]{1,0:T(8,128)(2,1)S(1)} %copy-done.5), channel_id=1, source_target_pairs={{0,4},{4,0},{8,12},{12,8},{1,5},{5,1},{9,13},{13,9},{2,6},{6,2},{1... | collective-permute-start | bytes 98312 | tf_op jit(solution)/shard_map/ppermute | solution.py:319
  16.6 1.9 %collective-permute-start.3 = (bf16[8,6272]{1,0:T(8,128)(2,1)S(1)}, bf16[8,6272]{1,0:T(8,128)(2,1)S(1)}, u32[]{:S(2)}, u32[]{:S(2)}) collective-permute-start(bf16[8,6272]{1,0:T(8,128)(2,1)S(1)} %get-tuple-element.23), channel_id=1, source_target_pairs={{0,1},{1,0},{2,3},{3,2},{4,5},{5,4},{6,7},{7,6},{8,9},{9,8},{10,11... | collective-permute-start | bytes 301064 | tf_op jit(solution)/shard_map/ppermute | solution.py:319
  16.7 5.8 %collective-permute-start.4 = (bf16[8,6272]{1,0:T(8,128)(2,1)S(1)}, bf16[8,6272]{1,0:T(8,128)(2,1)S(1)}, u32[]{:S(2)}, u32[]{:S(2)}) collective-permute-start(bf16[8,6272]{1,0:T(8,128)(2,1)S(1)} %get-tuple-element.24), channel_id=1, source_target_pairs={{0,2},{1,3},{2,0},{3,1},{4,6},{5,7},{6,4},{7,5},{8,10},{9,11},{10,... | collective-permute-start | bytes 301064 | tf_op jit(solution)/shard_map/ppermute | solution.py:319
  18.2 5.3 %collective-permute-start.5 = (bf16[8,6272]{1,0:T(8,128)(2,1)S(1)}, bf16[8,6272]{1,0:T(8,128)(2,1)S(1)}, u32[]{:S(2)}, u32[]{:S(2)}) collective-permute-start(bf16[8,6272]{1,0:T(8,128)(2,1)S(1)} %get-tuple-element.25), channel_id=1, source_target_pairs={{0,3},{1,2},{2,1},{3,0},{4,7},{5,6},{6,5},{7,4},{8,11},{9,10},{10,... | collective-permute-start | bytes 301064 | tf_op jit(solution)/shard_map/ppermute | solution.py:319
  24.8 3.4 %collective-permute-start.8 = (bf16[8,2048]{1,0:T(8,128)(2,1)S(1)}, bf16[8,2048]{1,0:T(8,128)(2,1)S(1)}, u32[]{:S(2)}, u32[]{:S(2)}) collective-permute-start(bf16[8,2048]{1,0:T(8,128)(2,1)S(1)} %shard_map.151.refs_0_), channel_id=1, source_target_pairs={{0,3},{1,2},{2,1},{3,0},{4,7},{5,6},{6,5},{7,4},{8,11},{9,10},{10,... | collective-permute-start | bytes 98312 | tf_op jit(solution)/shard_map/ppermute | solution.py:319
  26.3 3.9 %collective-permute-start.7 = (bf16[8,2048]{1,0:T(8,128)(2,1)S(1)}, bf16[8,2048]{1,0:T(8,128)(2,1)S(1)}, u32[]{:S(2)}, u32[]{:S(2)}) collective-permute-start(bf16[8,2048]{1,0:T(8,128)(2,1)S(1)} %shard_map.151.refs_0_), channel_id=1, source_target_pairs={{0,2},{1,3},{2,0},{3,1},{4,6},{5,7},{6,4},{7,5},{8,10},{9,11},{10,... | collective-permute-start | bytes 98312 | tf_op jit(solution)/shard_map/ppermute | solution.py:319
  26.8 3.4 %collective-permute-start.6 = (bf16[8,2048]{1,0:T(8,128)(2,1)S(1)}, bf16[8,2048]{1,0:T(8,128)(2,1)S(1)}, u32[]{:S(2)}, u32[]{:S(2)}) collective-permute-start(bf16[8,2048]{1,0:T(8,128)(2,1)S(1)} %shard_map.151.refs_0_), channel_id=1, source_target_pairs={{0,1},{1,0},{2,3},{3,2},{4,5},{5,4},{6,7},{7,6},{8,9},{9,8},{10,11... | collective-permute-start | bytes 98312 | tf_op jit(solution)/shard_map/ppermute | solution.py:319
  31.9 12.6 %collective-permute-start.11 = (bf16[32,2048]{1,0:T(8,128)(2,1)S(1)}, bf16[32,2048]{1,0:T(8,128)(2,1)S(1)}, u32[]{:S(2)}, u32[]{:S(2)}) collective-permute-start(bf16[32,2048]{1,0:T(8,128)(2,1)S(1)} %get-tuple-element.30), channel_id=1, source_target_pairs={{0,12},{4,8},{8,4},{12,0},{1,13},{5,9},{9,5},{13,1},{2,14},{6,10},... | collective-permute-start | bytes 393224 | tf_op jit(solution)/shard_map/ppermute | solution.py:319
  34.5 10.6 %collective-permute-start.10 = (bf16[32,2048]{1,0:T(8,128)(2,1)S(1)}, bf16[32,2048]{1,0:T(8,128)(2,1)S(1)}, u32[]{:S(2)}, u32[]{:S(2)}) collective-permute-start(bf16[32,2048]{1,0:T(8,128)(2,1)S(1)} %get-tuple-element.30), channel_id=1, source_target_pairs={{0,8},{4,12},{8,0},{12,4},{1,9},{5,13},{9,1},{13,5},{2,10},{6,14},... | collective-permute-start | bytes 393224 | tf_op jit(solution)/shard_map/ppermute | solution.py:319
  34.5 10.6 %collective-permute-start.9 = (bf16[32,2048]{1,0:T(8,128)(2,1)S(1)}, bf16[32,2048]{1,0:T(8,128)(2,1)S(1)}, u32[]{:S(2)}, u32[]{:S(2)}) collective-permute-start(bf16[32,2048]{1,0:T(8,128)(2,1)S(1)} %get-tuple-element.30), channel_id=1, source_target_pairs={{0,4},{4,0},{8,12},{12,8},{1,5},{5,1},{9,13},{13,9},{2,6},{6,2},{1... | collective-permute-start | bytes 393224 | tf_op jit(solution)/shard_map/ppermute | solution.py:319
  36.3 8.8 %copy-start.6 = (f32[2048]{0:T(1024)S(1)}, f32[2048]{0:T(1024)}, u32[]{:S(2)}) copy-start(f32[2048]{0:T(1024)} %param.22) | copy-start | bytes 24580
  44.5 12.6 %copy-start.1 = (bf16[2,3,8,2048]{3,2,1,0:T(8,128)(2,1)S(1)}, bf16[2,3,8,2048]{3,2,1,0:T(8,128)(2,1)}, u32[]{:S(2)}) copy-start(bf16[2,3,8,2048]{3,2,1,0:T(8,128)(2,1)} %refs_5_.1) | copy-start | bytes 589828
  44.5 12.6 %copy-start.2 = (f32[3,3,2048]{2,1,0:T(4,128)S(1)}, f32[3,3,2048]{2,1,0:T(4,128)}, u32[]{:S(2)}) copy-start(f32[3,3,2048]{2,1,0:T(4,128)} %refs_4_.3) | copy-start | bytes 221188
  44.5 12.6 %copy-start.3 = (bf16[2,8,2048]{2,1,0:T(8,128)(2,1)S(1)}, bf16[2,8,2048]{2,1,0:T(8,128)(2,1)}, u32[]{:S(2)}) copy-start(bf16[2,8,2048]{2,1,0:T(8,128)(2,1)} %refs_7_.1) | copy-start | bytes 196612
  44.6 12.6 %copy-start.4 = (f32[3,2048]{1,0:T(4,128)S(1)}, f32[3,2048]{1,0:T(4,128)}, u32[]{:S(2)}) copy-start(f32[3,2048]{1,0:T(4,128)} %refs_6_.3) | copy-start | bytes 73732
  50.2 1.9 %collective-permute-start.12 = (bf16[8,6272]{1,0:T(8,128)(2,1)S(1)}, bf16[8,6272]{1,0:T(8,128)(2,1)S(1)}, u32[]{:S(2)}, u32[]{:S(2)}) collective-permute-start(bf16[8,6272]{1,0:T(8,128)(2,1)S(1)} %get-tuple-element.33), channel_id=1, source_target_pairs={{0,1},{1,0},{2,3},{3,2},{4,5},{5,4},{6,7},{7,6},{8,9},{9,8},{10,11... | collective-permute-start | bytes 301064 | tf_op jit(solution)/shard_map/ppermute | solution.py:319
  50.2 5.7 %collective-permute-start.13 = (bf16[8,6272]{1,0:T(8,128)(2,1)S(1)}, bf16[8,6272]{1,0:T(8,128)(2,1)S(1)}, u32[]{:S(2)}, u32[]{:S(2)}) collective-permute-start(bf16[8,6272]{1,0:T(8,128)(2,1)S(1)} %get-tuple-element.34), channel_id=1, source_target_pairs={{0,2},{1,3},{2,0},{3,1},{4,6},{5,7},{6,4},{7,5},{8,10},{9,11},{10,... | collective-permute-start | bytes 301064 | tf_op jit(solution)/shard_map/ppermute | solution.py:319
  51.1 6.1 %collective-permute-start.14 = (bf16[8,6272]{1,0:T(8,128)(2,1)S(1)}, bf16[8,6272]{1,0:T(8,128)(2,1)S(1)}, u32[]{:S(2)}, u32[]{:S(2)}) collective-permute-start(bf16[8,6272]{1,0:T(8,128)(2,1)S(1)} %get-tuple-element.35), channel_id=1, source_target_pairs={{0,3},{1,2},{2,1},{3,0},{4,7},{5,6},{6,5},{7,4},{8,11},{9,10},{10,... | collective-permute-start | bytes 301064 | tf_op jit(solution)/shard_map/ppermute | solution.py:319
